TPU v7x, 128 devices: a whole 4x4x4 slice. The times are simulated.
128 devices in a mesh: tm: 2 (over core), cls: 64 (over z, x, y).
Axes of the slice: x: 4, y: 4, z: 4, core: 2. Of those that a mesh axis runs over, the one named last changes fastest.
Arguments:
- visibilities: bfloat16 [32768, 3072], P(('tm', 'cls')), may hold values from -6 to 6
- row_class: int32 [32768, 1], P(('tm', 'cls')), may hold values from 0 to 255; in each aligned block of 256 rows (0 to 255, 256 to 511, ...) at most 2 rows name the same one
- filters: bfloat16 [256, 1536, 1536], P(('tm', 'cls'))
- flags: int32 [256, 1536], P(('tm', 'cls')), may hold values 0 or 1
- taper: float32 [1536], replicated, may hold values from 0.2 to 1
- pairs: int32 [32768, 2], P(('tm', 'cls')), may hold values from 0 to 32767, as said below
Outputs:
- power: float32 [32768, 1536], P(('tm', 'cls'))
Inputs may be any that keep to these rules, and one draw needn't show every extreme that they name: `row_class`: among the rows of one device at most 2 have any one class, and some class has exactly 2 of them. `pairs`: both entries of row p name rows of the same aligned block of 256 rows as p; the first column is a permutation of that block.
All inputs are finite; a program needn't handle non-finite values. No bound on the sum of `flags` on one device may be relied on, other than what follows from the above.
Results may differ from a plain program's by a relative error of at most 0.0068.
Values may be sent and summed in bfloat16 or wider, within the bound.
No kernel may reach another device: no remote copies, remote signals or barrier semaphores. Data moves between devices by JAX's collectives and lax.ppermute only.
A program may use at most 128 MiB of HBM per device.

v0:
```python
import math

import jax
import jax.numpy as jnp
from jax import lax
from jax.sharding import PartitionSpec as P


def dft_tables(width):
    index = jnp.arange(width, dtype=jnp.int32)
    phase = index[:, None] * index[None, :] % width
    angle = phase.astype(jnp.float32) * (2.0 * math.pi / width)
    scale = 1.0 / math.sqrt(width)
    return (
        (jnp.cos(angle) * scale).astype(jnp.bfloat16),
        (jnp.sin(angle) * scale).astype(jnp.bfloat16),
    )


def transform(block, keep, matrix, taper, cosines, sines):
    width = matrix.shape[0]
    count = block.shape[0]
    stacked = jnp.concatenate([block[:, :width], block[:, width:]], axis=0) * keep[None, :]
    filtered = jnp.dot(stacked, matrix, preferred_element_type=jnp.float32)
    tapered = (filtered * taper[None, :]).astype(jnp.bfloat16)
    along_cos = jnp.dot(tapered, cosines, preferred_element_type=jnp.float32)
    along_sin = jnp.dot(tapered, sines, preferred_element_type=jnp.float32)
    real_part = along_cos[:count] + along_sin[count:]
    imag_part = along_cos[count:] - along_sin[:count]
    return jnp.concatenate([real_part, imag_part], axis=1).astype(jnp.bfloat16)


def local(visibilities, row_class, filters, flags, taper, pairs):
    row_count = visibilities.shape[0]
    row_width = visibilities.shape[1]
    width = filters.shape[1]
    local_classes = filters.shape[0]
    devices = lax.axis_size(("tm", "cls"))
    total_classes = local_classes * devices
    capacity = max(2, 2 * row_count // total_classes)
    labels = row_class[:, 0]
    onehot = (labels[:, None] == jnp.arange(total_classes, dtype=jnp.int32)[None, :]).astype(
        jnp.int32
    )
    slot = jnp.sum(onehot * (jnp.cumsum(onehot, axis=0) - 1), axis=1)
    position = labels * capacity + slot
    outgoing = (
        jnp.zeros((total_classes * capacity, row_width), jnp.bfloat16)
        .at[position]
        .set(visibilities)
    )
    arrived = lax.all_to_all(
        outgoing.reshape(devices, local_classes * capacity, row_width),
        ("tm", "cls"),
        split_axis=0,
        concat_axis=0,
        tiled=True,
    )
    arrived = arrived.reshape(devices, local_classes, capacity, row_width)
    cosines, sines = dft_tables(width)
    keep_all = (1 - flags).astype(jnp.bfloat16)
    results = []
    for which in range(local_classes):
        block = arrived[:, which].reshape(devices * capacity, row_width)
        done = transform(block, keep_all[which], filters[which], taper, cosines, sines)
        results.append(done.reshape(devices, 1, capacity, row_width))
    finished = jnp.concatenate(results, axis=1)
    returned = lax.all_to_all(
        finished.reshape(devices, local_classes * capacity, row_width),
        ("tm", "cls"),
        split_axis=0,
        concat_axis=0,
        tiled=True,
    )
    returned = returned.reshape(total_classes * capacity, row_width)
    spectra = returned[position].astype(jnp.float32)
    offset = lax.axis_index(("tm", "cls")) * row_count
    first = spectra[pairs[:, 0] - offset]
    second = spectra[pairs[:, 1] - offset]
    return first[:, :width] * second[:, :width] + first[:, width:] * second[:, width:]


def solution(mesh):
    placed = (
        P(("tm", "cls"), None),
        P(("tm", "cls"), None),
        P(("tm", "cls"), None, None),
        P(("tm", "cls"), None),
        P(),
        P(("tm", "cls"), None),
    )
    return jax.shard_map(
        local, mesh=mesh, in_specs=placed, out_specs=P(("tm", "cls"), None), check_vma=False
    )
```

profile of v0, /device:TPU:4, one launch (start us, length us, event | category | flops | bytes accessed | tf_op | source)
XLA Modules:
  0.0 320.3 jit_solution(18416432379901342568)
XLA Ops:
  0.0 0.8 copy.15
  1.2 0.9 fusion.41
  2.1 0.7 compare_select_fusion.2
  2.7 4.7 %scatter_custom_fusion = bf16[512,3072]{1,0:T(8,128)(2,1)S(1)} fusion(s32[256]{0:T(256)S(1)} %bitcast.39, bf16[256,3072]{1,0:T(8,128)(2,1)} %param.6, bf16[]{:T(256)} %constant.14.clone.1), kind=kCustom, calls=%fused_computation.45 | custom fusion | bytes 3146240 | tf_op jit(solution)/shard_map/scatter | solution.py:50
  7.4 2.7 reshape.97
  10.1 11.1 %all-to-all-start = ((bf16[128,4,3072]{2,1,0:T(4,128)(2,1)}), bf16[128,4,3072]{2,1,0:T(4,128)(2,1)S(1)}, u32[]{:S(2)}, u32[]{:S(2)}) async-start(bf16[128,4,3072]{2,1,0:T(4,128)(2,1)} %reshape.97), calls=%async_computation | async-start | bytes 6291456 | tf_op jit(solution)/shard_map/all_to_all | solution.py:52
  21.4 41.6 %all-to-all-done = bf16[128,4,3072]{2,1,0:T(4,128)(2,1)S(1)} async-done(((bf16[128,4,3072]{2,1,0:T(4,128)(2,1)}), bf16[128,4,3072]{2,1,0:T(4,128)(2,1)S(1)}, u32[]{:S(2)}, u32[]{:S(2)}) %all-to-all-start) | async-done | bytes 3145760 | tf_op jit(solution)/shard_map/all_to_all | solution.py:52
  63.0 2.7 reshape.98
  65.7 4.8 %fusion.62 = (bf16[128,1,2,3072]{3,2,1,0:T(2,128)(2,1)}, bf16[128,1,2,3072]{3,2,1,0:T(2,128)(2,1)S(1)}) fusion(bf16[128,2,2,3072]{3,2,1,0:T(2,128)(2,1)} %reshape.98), kind=kLoop, calls=%fused_computation.85 | loop fusion | bytes 6291456 | tf_op jit(solution)/shard_map/slice | solution.py:64
  70.5 3.7 %reshape_squeeze.6 = bf16[256,3072]{1,0:T(8,128)(2,1)S(1)} reshape(bf16[128,1,2,3072]{3,2,1,0:T(2,128)(2,1)} %get-tuple-element.11) | data formatting | bytes 3145728 | tf_op jit(solution)/shard_map/reshape;squeeze | solution.py:64
  74.3 4.9 %fusion.24 = bf16[512,1536]{1,0:T(8,128)(2,1)S(1)} fusion(bf16[2,1536,1536]{2,1,0:T(8,128)(2,1)} %param.8, bf16[256,1536]{1,0:T(8,128)(2,1)S(1)} %get-tuple-element.14, bf16[256,1536]{1,0:T(8,128)(2,1)S(1)} %get-tuple-element.13, f32[1536]{0:T(1024)S(1)} %copy-done.4, bf16[1536]{0:T(1024)(128)(2,1)S(1)} %get-tuple-element.5), kind=kOutput, calls=%fused_computation.27 | convolution fusion | flops 2422210560 | bytes 7873536 | tf_op jit(solution)/shard_map/dot_general | solution.py:24
  79.3 38.1 %fusion.11 = f32[512,1536]{1,0:T(8,128)} fusion(bf16[512,1536]{1,0:T(8,128)(2,1)S(1)} %fusion.24), kind=kOutput, calls=%fused_computation.19 | convolution fusion | flops 2441871360 | bytes 4718592 | tf_op jit(solution)/shard_map/dot_general | solution.py:26
  117.3 38.6 %fusion.13 = f32[512,1536]{1,0:T(8,128)} fusion(bf16[512,1536]{1,0:T(8,128)(2,1)S(1)} %fusion.24), kind=kOutput, calls=%fused_computation.21 | convolution fusion | flops 2441871360 | bytes 4718592 | tf_op jit(solution)/shard_map/dot_general | solution.py:27
  155.9 0.6 reshape_squeeze.7
  156.7 4.9 %fusion.21 = bf16[512,1536]{1,0:T(8,128)(2,1)S(1)} fusion(bf16[2,1536,1536]{2,1,0:T(8,128)(2,1)} %param.8, bf16[256,1536]{1,0:T(8,128)(2,1)S(1)} %get-tuple-element.16, bf16[256,1536]{1,0:T(8,128)(2,1)S(1)} %get-tuple-element.15, f32[1536]{0:T(1024)S(1)} %copy-done.4, bf16[1536]{0:T(1024)(128)(2,1)S(1)} %get-tuple-element.6), kind=kOutput, calls=%fused_computation.26 | convolution fusion | flops 2422210560 | bytes 7873536 | tf_op jit(solution)/shard_map/dot_general | solution.py:24
  161.6 38.1 %fusion.10 = f32[512,1536]{1,0:T(8,128)} fusion(bf16[512,1536]{1,0:T(8,128)(2,1)S(1)} %fusion.21), kind=kOutput, calls=%fused_computation.18 | convolution fusion | flops 2441871360 | bytes 4718592 | tf_op jit(solution)/shard_map/dot_general | solution.py:26
  199.7 38.6 %fusion.12 = f32[512,1536]{1,0:T(8,128)} fusion(bf16[512,1536]{1,0:T(8,128)(2,1)S(1)} %fusion.21), kind=kOutput, calls=%fused_computation.20 | convolution fusion | flops 2441871360 | bytes 4718592 | tf_op jit(solution)/shard_map/dot_general | solution.py:27
  238.3 0.7 fusion.31
  239.0 0.3 concatenate.40
  239.4 0.3 concatenate.41
  239.8 4.2 %fusion.29 = (bf16[256,1536]{1,0:T(8,128)(2,1)S(1)}, bf16[256,1536]{1,0:T(8,128)(2,1)}) fusion(f32[512,1536]{1,0:T(8,128)} %fusion.12, f32[512,1536]{1,0:T(8,128)} %fusion.10), kind=kLoop, calls=%fused_computation.34 | loop fusion | flops 1572864 | bytes 7864320 | tf_op jit(solution)/shard_map/convert.3
  244.4 2.2 concatenate.45
  246.6 0.7 maximum_maximum_fusion
  247.4 4.1 %copy.21 = bf16[128,4,3072]{2,1,0:T(4,128)(2,1)} copy(bf16[128,4,3072]{2,0,1:T(8,128)(2,1)S(1)} %bitcast.35) | data formatting | bytes 6291456 | tf_op jit(solution)/shard_map/reshape | solution.py:69
  251.5 6.6 %all-to-all-start.1 = ((bf16[128,4,3072]{2,1,0:T(4,128)(2,1)}), bf16[128,4,3072]{2,1,0:T(4,128)(2,1)}, u32[]{:S(2)}, u32[]{:S(2)}) async-start(bf16[128,4,3072]{2,1,0:T(4,128)(2,1)} %copy.21), calls=%async_computation.1 | async-start | bytes 6291456 | tf_op jit(solution)/shard_map/all_to_all | solution.py:68
  258.2 41.5 %all-to-all-done.1 = bf16[128,4,3072]{2,1,0:T(4,128)(2,1)} async-done(((bf16[128,4,3072]{2,1,0:T(4,128)(2,1)}), bf16[128,4,3072]{2,1,0:T(4,128)(2,1)}, u32[]{:S(2)}, u32[]{:S(2)}) %all-to-all-start.1) | async-done | bytes 3145760 | tf_op jit(solution)/shard_map/all_to_all | solution.py:68
  299.6 4.5 %reshape.100 = bf16[512,3072]{1,0:T(8,128)(2,1)S(1)} reshape(bf16[128,4,3072]{2,1,0:T(4,128)(2,1)} %all-to-all-done.1) | data formatting | bytes 6291456 | tf_op jit(solution)/shard_map/reshape | solution.py:75
  304.1 2.7 gather_fusion
  306.8 1.8 convert_element_type.59
  308.6 3.4 %gather_fusion.1 = f32[256,3072]{1,0:T(8,128)} fusion(f32[256,3072]{1,0:T(8,128)S(1)} %convert_element_type.59, s32[1024]{0:T(1024)S(1)} %pad_clamp_fusion.1), kind=kCustom, calls=%fused_computation.1 | custom fusion | bytes 6292480 | tf_op jit(solution)/shard_map/gather | solution.py:78
  312.0 3.3 %gather_fusion.2 = f32[256,3072]{1,0:T(8,128)} fusion(f32[256,3072]{1,0:T(8,128)S(1)} %convert_element_type.59, s32[1024]{0:T(1024)S(1)} %pad_clamp_fusion), kind=kCustom, calls=%fused_computation.2 | custom fusion | bytes 6292480 | tf_op jit(solution)/shard_map/gather | solution.py:79
  315.3 4.6 %fusion.27 = f32[256,1536]{1,0:T(8,128)} fusion(f32[256,3072]{1,0:T(8,128)} %gather_fusion.2, f32[256,3072]{1,0:T(8,128)} %gather_fusion.1), kind=kLoop, calls=%fused_computation.29 | loop fusion | flops 1179648 | bytes 7864320 | tf_op jit(solution)/shard_map/add | solution.py:80
  (29 shorter events, 1.3 us)
Async XLA Ops:
  10.1 11.1 %copy-start.2 = (s32[2,1536]{1,0:T(2,128)S(1)}, s32[2,1536]{1,0:T(2,128)}, u32[]{:S(2)}) copy-start(s32[2,1536]{1,0:T(2,128)} %param.9) | copy-start | bytes 36868
  10.1 52.9 %all-to-all-start = ((bf16[128,4,3072]{2,1,0:T(4,128)(2,1)}), bf16[128,4,3072]{2,1,0:T(4,128)(2,1)S(1)}, u32[]{:S(2)}, u32[]{:S(2)}) async-start(bf16[128,4,3072]{2,1,0:T(4,128)(2,1)} %reshape.97), calls=%async_computation | async-start | bytes 6291456 | tf_op jit(solution)/shard_map/all_to_all | solution.py:52
  70.5 3.8 %copy-start.4 = (f32[1536]{0:T(1024)S(1)}, f32[1536]{0:T(1024)}, u32[]{:S(2)}) copy-start(f32[1536]{0:T(1024)} %param.10) | copy-start | bytes 18436
  199.7 38.6 %copy-start = (f32[512,1536]{1,0:T(8,128)S(1)}, f32[512,1536]{1,0:T(8,128)}, u32[]{:S(2)}) copy-start(f32[512,1536]{1,0:T(8,128)} %fusion.11) | copy-start | bytes 9437188
  199.7 38.6 %copy-start.1 = (f32[512,1536]{1,0:T(8,128)S(1)}, f32[512,1536]{1,0:T(8,128)}, u32[]{:S(2)}) copy-start(f32[512,1536]{1,0:T(8,128)} %fusion.13) | copy-start | bytes 9437188
  251.5 6.6 %copy-start.3 = (s32[256,2]{0,1:T(2,128)S(1)}, s32[256,2]{0,1:T(2,128)}, u32[]{:S(2)}) copy-start(s32[256,2]{0,1:T(2,128)} %param.11) | copy-start | bytes 6148
  251.5 48.1 %all-to-all-start.1 = ((bf16[128,4,3072]{2,1,0:T(4,128)(2,1)}), bf16[128,4,3072]{2,1,0:T(4,128)(2,1)}, u32[]{:S(2)}, u32[]{:S(2)}) async-start(bf16[128,4,3072]{2,1,0:T(4,128)(2,1)} %copy.21), calls=%async_computation.1 | async-start | bytes 6291456 | tf_op jit(solution)/shard_map/all_to_all | solution.py:68
where the time goes:
time: 325 us; the launch traced here: 320 us
  matrix products  163 us (50%)
  waiting for transfers between devices  83.1 us (26%)
  local copies, waits for them, and re-layouts  41.7 us (13%)
  starting transfers between devices  17.7 us (5%)
  other arithmetic  13.9 us (4%)
    dot_general x2, matrix products, transform(): along_sin = jnp.dot(tapered, sines, preferred_element_type=jnp.float32)  77.1 us
    dot_general x2, matrix products, transform(): along_cos = jnp.dot(tapered, cosines, preferred_element_type=jnp.float32)  76.2 us
    all_to_all x1, waiting for transfers between devices, local(): lax.all_to_all(outgoing.reshape(devices, local_classes * capacity, row_wi...  41.6 us
    all_to_all x1, waiting for transfers between devices, local(): lax.all_to_all(finished.reshape(devices, local_classes * capacity, row_wi...  41.5 us
    all_to_all x1, starting transfers between devices, local(): lax.all_to_all(outgoing.reshape(devices, local_classes * capacity, row_wi...  11.1 us
    dot_general x2, matrix products, transform(): filtered = jnp.dot(stacked, matrix, preferred_element_type=jnp.float32)  9.88 us
    all_to_all x1, starting transfers between devices, local(): lax.all_to_all(finished.reshape(devices, local_classes * capacity, row_wi...  6.58 us
  transfers between devices with their start and end apart: 2, of which 2 were waited for; matrix products, arithmetic and copies ran while one was open for 0% of the time, Pallas kernels for 0%

commit v1 on v0

v1 whole, which is shorter than its diff:
```python
import math

import jax
import jax.numpy as jnp
from jax import lax
from jax.experimental import pallas as pl
from jax.experimental.pallas import tpu as pltpu
from jax.sharding import PartitionSpec as P

BF16 = jnp.bfloat16
F32 = jnp.float32
SLOTS = 2
PARTS = 2
TILE = 8
LIMIT = 48 << 20


def iota(shape, axis):
    return lax.broadcasted_iota(jnp.int32, shape, axis)


def row_of_slot(labels_row):
    count = labels_row.shape[1]
    across = jnp.broadcast_to(labels_row.astype(F32), (count, count))
    down = across.T
    earlier = iota((count, count), 0) < iota((count, count), 1)
    slot = jnp.sum(jnp.where((across == down) & earlier, 1.0, 0.0), axis=0, keepdims=True)
    slot = slot.astype(jnp.int32)
    return (labels_row >> 1) * TILE + (labels_row & 1) * (PARTS * SLOTS) + slot


def pack_kernel(labels_ref, real_ref, imag_ref, out_ref, select_ref):
    rows = out_ref.shape[0]
    count = real_ref.shape[0]

    @pl.when(pl.program_id(0) == 0)
    def _():
        place = row_of_slot(labels_ref[...])
        index = iota((rows, count), 0)
        select_ref[:, :count] = jnp.where(index == place, 1.0, 0.0).astype(BF16)
        select_ref[:, count:] = jnp.where(index == place + SLOTS, 1.0, 0.0).astype(BF16)

    stacked = jnp.concatenate([real_ref[...], imag_ref[...]], axis=0)
    out_ref[...] = jnp.dot(select_ref[...], stacked, preferred_element_type=F32).astype(BF16)


def pack(labels_row, visibilities, rows, width, step):
    count = visibilities.shape[0]
    steps = width // step
    return pl.pallas_call(
        pack_kernel,
        grid=(steps,),
        in_specs=[
            pl.BlockSpec((1, count), lambda j: (0, 0)),
            pl.BlockSpec((count, step), lambda j: (0, j)),
            pl.BlockSpec((count, step), lambda j: (0, j + steps)),
        ],
        out_specs=pl.BlockSpec((rows, step), lambda j: (0, j)),
        out_shape=jax.ShapeDtypeStruct((rows, width), BF16),
        scratch_shapes=[pltpu.VMEM((rows, PARTS * count), BF16)],
        compiler_params=pltpu.CompilerParams(vmem_limit_bytes=LIMIT),
        name="pack",
    )(labels_row, visibilities, visibilities)


def index_kernel(labels_ref, pairs_ref, fetch_ref, second_ref):
    count = labels_ref.shape[1]
    rows = fetch_ref.shape[1]
    place = row_of_slot(labels_ref[...])
    local = (pairs_ref[...] & (count - 1)).astype(F32)
    first = jnp.broadcast_to(local[0:1], (count, count))
    other = jnp.broadcast_to(local[1:2], (count, count))
    first_down = first.T.astype(jnp.int32)
    lane = iota((count, count), 1)
    source = jnp.sum(
        jnp.where(first_down == lane, place.astype(F32), 0.0), axis=1, keepdims=True
    ).astype(jnp.int32)
    index = iota((count, rows), 1)
    fetch_ref[:count, :] = jnp.where(index == source, 1.0, 0.0).astype(BF16)
    fetch_ref[count:, :] = jnp.where(index == source + SLOTS, 1.0, 0.0).astype(BF16)
    second_ref[...] = jnp.where(other.T == first, 1.0, 0.0).astype(BF16)


def indices(labels_row, pairs_rows, rows):
    count = labels_row.shape[1]
    return pl.pallas_call(
        index_kernel,
        out_shape=(
            jax.ShapeDtypeStruct((PARTS * count, rows), BF16),
            jax.ShapeDtypeStruct((count, count), BF16),
        ),
        compiler_params=pltpu.CompilerParams(vmem_limit_bytes=LIMIT),
        name="indices",
    )(labels_row, pairs_rows)


def table_kernel(coarse_cos_ref, coarse_sin_ref, fine_cos_ref, fine_sin_ref, cos_ref, sin_ref):
    fine = fine_cos_ref.shape[0]
    fine_cos, fine_sin = fine_cos_ref[...], fine_sin_ref[...]
    for i in range(cos_ref.shape[0] // fine):
        coarse_cos, coarse_sin = coarse_cos_ref[i : i + 1, :], coarse_sin_ref[i : i + 1, :]
        at = pl.ds(i * fine, fine)
        cos_ref[at, :] = (coarse_cos * fine_cos - coarse_sin * fine_sin).astype(BF16)
        sin_ref[at, :] = (coarse_sin * fine_cos + coarse_cos * fine_sin).astype(BF16)


def dft_tables(width, fine, step):
    def angles(rows, spacing):
        n = jnp.arange(rows, dtype=jnp.int32) * spacing
        phase = n[:, None] * jnp.arange(width, dtype=jnp.int32)[None, :] % width
        return phase.astype(F32) * (2.0 * math.pi / width)

    coarse, small = angles(width // fine, fine), angles(fine, 1)
    scale = 1.0 / math.sqrt(width)
    whole = lambda rows: pl.BlockSpec((rows, step), lambda j: (0, j))
    return pl.pallas_call(
        table_kernel,
        grid=(width // step,),
        in_specs=[whole(width // fine), whole(width // fine), whole(fine), whole(fine)],
        out_specs=(whole(width), whole(width)),
        out_shape=(jax.ShapeDtypeStruct((width, width), BF16),) * 2,
        compiler_params=pltpu.CompilerParams(vmem_limit_bytes=LIMIT),
        name="tables",
    )(jnp.cos(coarse) * scale, jnp.sin(coarse) * scale, jnp.cos(small), jnp.sin(small))


def filter_kernel(arrived_ref, flags_ref, taper_ref, filters_ref, out_ref, masked_ref):
    rows, width = arrived_ref.shape
    step = out_ref.shape[1]
    half = TILE // 2

    @pl.when(pl.program_id(0) == 0)
    def _():
        keep = (1 - flags_ref[...]).astype(F32)
        arrived = arrived_ref[...].astype(F32).reshape(rows // (2 * TILE), 2, TILE, width)
        even, odd = arrived[:, 0], arrived[:, 1]
        low = iota((1, TILE, 1), 1) < half
        first = jnp.where(low, even, pltpu.roll(odd, half, 1)) * keep[0:1][None]
        second = jnp.where(low, pltpu.roll(even, half, 1), odd) * keep[1:2][None]
        masked_ref[0] = first.reshape(rows // 2, width).astype(BF16)
        masked_ref[1] = second.reshape(rows // 2, width).astype(BF16)

    taper = taper_ref[...]
    tiled = (rows // (2 * TILE), TILE, step)
    done = [
        (jnp.dot(masked_ref[w], filters_ref[w], preferred_element_type=F32) * taper).reshape(tiled)
        for w in range(2)
    ]
    low = iota((1, TILE, 1), 1) < half
    even = jnp.where(low, done[0], pltpu.roll(done[1], half, 1))
    odd = jnp.where(low, pltpu.roll(done[0], half, 1), done[1])
    both = jnp.concatenate([even[:, None], odd[:, None]], axis=1)
    out_ref[...] = both.reshape(rows, step).astype(BF16)


def filter_rows(arrived, flags, taper_row, filters, step):
    rows, width = arrived.shape
    return pl.pallas_call(
        filter_kernel,
        grid=(width // step,),
        in_specs=[
            pl.BlockSpec((rows, width), lambda j: (0, 0), pipeline_mode=pl.Buffered(1)),
            pl.BlockSpec((2, width), lambda j: (0, 0)),
            pl.BlockSpec((1, step), lambda j: (0, j)),
            pl.BlockSpec((2, width, step), lambda j: (0, 0, j)),
        ],
        out_specs=pl.BlockSpec((rows, step), lambda j: (0, j)),
        out_shape=jax.ShapeDtypeStruct((rows, width), BF16),
        scratch_shapes=[pltpu.VMEM((2, rows // 2, width), BF16)],
        compiler_params=pltpu.CompilerParams(vmem_limit_bytes=LIMIT),
        name="filter",
    )(arrived, flags, taper_row, filters)


def power_kernel(returned_ref, fetch_ref, second_ref, cos_ref, sin_ref, out_ref, tapered_ref):
    count = second_ref.shape[0]

    @pl.when(pl.program_id(0) == 0)
    def _():
        tapered_ref[...] = jnp.dot(
            fetch_ref[...], returned_ref[...], preferred_element_type=F32
        ).astype(BF16)

    tapered = tapered_ref[...]
    along_cos = jnp.dot(tapered, cos_ref[...], preferred_element_type=F32)
    along_sin = jnp.dot(tapered, sin_ref[...], preferred_element_type=F32)
    real = (along_cos[:count] + along_sin[count:]).astype(BF16)
    imag = (along_cos[count:] - along_sin[:count]).astype(BF16)
    second = second_ref[...]
    other_real = jnp.dot(second, real, preferred_element_type=F32)
    other_imag = jnp.dot(second, imag, preferred_element_type=F32)
    out_ref[...] = real.astype(F32) * other_real + imag.astype(F32) * other_imag


def cross_power(returned, fetch, second, cosines, sines, step):
    rows, width = returned.shape
    count = second.shape[0]
    once = lambda shape: pl.BlockSpec(shape, lambda j: (0, 0), pipeline_mode=pl.Buffered(1))
    column = lambda height: pl.BlockSpec((height, step), lambda j: (0, j))
    return pl.pallas_call(
        power_kernel,
        grid=(width // step,),
        in_specs=[
            once((rows, width)),
            once(fetch.shape),
            once(second.shape),
            column(width),
            column(width),
        ],
        out_specs=column(count),
        out_shape=jax.ShapeDtypeStruct((count, width), F32),
        scratch_shapes=[pltpu.VMEM((PARTS * count, width), BF16)],
        compiler_params=pltpu.CompilerParams(vmem_limit_bytes=LIMIT),
        name="power",
    )(returned, fetch, second, cosines, sines)


def exchange(packed, peers):
    rows, width = packed.shape
    moved = lax.all_to_all(
        packed.reshape(peers, rows // peers, width),
        ("tm", "cls"),
        split_axis=0,
        concat_axis=0,
        tiled=True,
    )
    return moved.reshape(rows, width)


def local(visibilities, row_class, filters, flags, taper, pairs):
    count = visibilities.shape[0]
    classes, width = filters.shape[0], filters.shape[1]
    peers = lax.axis_size(("tm", "cls"))
    rows = peers * TILE
    assert classes == 2 and count & (count - 1) == 0
    labels_row = row_class.reshape(1, count)
    packed = pack(labels_row, visibilities, rows, width, 512)
    arrived = exchange(packed, peers)
    fetch, second = indices(labels_row, pairs.T, rows)
    cosines, sines = dft_tables(width, 32, 256)
    tapered = filter_rows(arrived, flags, taper.reshape(1, width), filters, 256)
    returned = exchange(tapered, peers)
    return cross_power(returned, fetch, second, cosines, sines, 256)


def solution(mesh):
    across = ("tm", "cls")
    placed = (
        P(across, None),
        P(across, None),
        P(across, None, None),
        P(across, None),
        P(),
        P(across, None),
    )
    return jax.shard_map(
        local, mesh=mesh, in_specs=placed, out_specs=P(across, None), check_vma=False
    )
```

time: 325 us -> 134 us (0.41); the launches traced: 320 us -> 133 us
  matrix products: 163 us -> 0 us
  local copies, waits for them, and re-layouts: 41.7 us -> 8.12 us
  Pallas kernels: 0 us -> 33.3 us
  other arithmetic: 13.9 us -> 2.1 us
  waiting for transfers between devices: 83.1 us -> 73.3 us
    dot_general x6 -> x0, matrix products: 163 us -> none  [the longest x2 77.1 us: transform(): along_sin = jnp.dot(tapered, sines, preferred_element_type=jnp.float32)]
    pallas_call x0 -> x5, Pallas kernels: none -> 33.3 us  [the longest x1 12.2 us: cross_power(): pl.pallas_call(power_kernel, grid=(width // step,), in_specs=[once((rows,...]
    reshape x4 -> x1, local copies, waits for them, and re-layouts: 14 us -> 0.01 us  [local(): tapered = filter_rows(arrived, flags, taper.reshape(1, width), filters, 256)]
    all_to_all x2, waiting for transfers between devices: 83.1 us -> 73.3 us  [exchange(): lax.all_to_all(packed.reshape(peers, rows // peers, width), ('tm', 'cls')...]
    gather x3 -> x0, local copies, waits for them, and re-layouts: 9.43 us -> none  [the longest x1 3.38 us: local(): first = spectra[pairs[:, 0] - offset]]
    unnamed x10 -> x20, local copies, waits for them, and re-layouts: 0.02 us -> 8.11 us
    another operation x4 -> x0, other arithmetic: 5.16 us -> none
    slice x4 -> x0, local copies, waits for them, and re-layouts: 5.11 us -> none  [the longest x1 4.85 us: local(): block = arrived[:, which].reshape(devices * capacity, row_width)]
  transfers between devices with their start and end apart: 2 -> 2, of which waited for: 2 -> 2; matrix products, arithmetic and copies ran while one was open for 0% -> 2% of each run, Pallas kernels for 0% -> 4%
where the time goes in v1:
time: 134 us; the launch traced here: 133 us
  waiting for transfers between devices  73.3 us (55%)
  Pallas kernels  33.3 us (25%)
  starting transfers between devices  16.6 us (12%)
  local copies, waits for them, and re-layouts  8.12 us (6%)
  other arithmetic  2.1 us (2%)
    all_to_all x2, waiting for transfers between devices, exchange(): lax.all_to_all(packed.reshape(peers, rows // peers, width), ('tm', 'cls')...  73.3 us
    all_to_all x2, starting transfers between devices, exchange(): lax.all_to_all(packed.reshape(peers, rows // peers, width), ('tm', 'cls')...  16.6 us
    pallas_call x1, Pallas kernels, cross_power(): pl.pallas_call(power_kernel, grid=(width // step,), in_specs=[once((rows,...  12.2 us
    pallas_call x1, Pallas kernels, filter_rows(): pl.pallas_call(filter_kernel, grid=(width // step,), in_specs=[pl.BlockSp...  11.8 us
    unnamed x20, local copies, waits for them, and re-layouts  8.11 us
    pallas_call x1, Pallas kernels, dft_tables(): pl.pallas_call(table_kernel, grid=(width // step,), in_specs=[whole(width...  4.67 us
    pallas_call x1, Pallas kernels, pack(): pl.pallas_call(pack_kernel, grid=(steps,), in_specs=[pl.BlockSpec((1, cou...  4.19 us
  transfers between devices with their start and end apart: 2, of which 2 were waited for; matrix products, arithmetic and copies ran while one was open for 2% of the time, Pallas kernels for 4%

profile of v1, /device:TPU:4, one launch (start us, length us, event | category | flops | bytes accessed | tf_op | source)
XLA Modules:
  0.0 133.4 jit_solution(14687475626628110210)
XLA Ops:
  0.0 0.0 copy-start
  0.0 1.4 %copy-done = bf16[256,3072]{1,0:T(8,128)(2,1)S(1)} copy-done((bf16[256,3072]{1,0:T(8,128)(2,1)S(1)}, bf16[256,3072]{1,0:T(8,128)(2,1)}, u32[]{:S(2)}) %copy-start) | copy-done | bytes 1572888
  1.4 0.0 copy-start.5
  1.4 0.7 copy-done.5
  2.1 4.2 %pack.1 = bf16[1024,1536]{1,0:T(8,128)(2,1)} custom-call(s32[1,256]{1,0:T(1,128)S(1)} %bitcast.7, bf16[256,3072]{1,0:T(8,128)(2,1)S(1)} %copy-done, bf16[256,3072]{1,0:T(8,128)(2,1)S(1)} %copy-done), custom_call_target="tpu_custom_call" | custom-call | tf_op jit(solution)/shard_map/pack/pallas_call | solution.py:50
  6.3 0.0 copy-start.9
  6.3 0.0 copy-start.4
  6.3 10.5 %all-to-all-start = ((bf16[128,8,1536]{2,1,0:T(8,128)(2,1)}), bf16[128,8,1536]{2,1,0:T(8,128)(2,1)S(1)}, u32[]{:S(2)}, u32[]{:S(2)}) async-start(bf16[128,8,1536]{2,1,0:T(8,128)(2,1)} %bitcast.1), calls=%async_computation | async-start | bytes 6291456 | tf_op jit(solution)/shard_map/all_to_all | solution.py:220
  16.8 0.0 copy-done.9
  16.8 41.8 %all-to-all-done = bf16[128,8,1536]{2,1,0:T(8,128)(2,1)S(1)} async-done(((bf16[128,8,1536]{2,1,0:T(8,128)(2,1)}), bf16[128,8,1536]{2,1,0:T(8,128)(2,1)S(1)}, u32[]{:S(2)}, u32[]{:S(2)}) %all-to-all-start) | async-done | bytes 3145760 | tf_op jit(solution)/shard_map/all_to_all | solution.py:220
  58.6 0.0 copy-start.8
  58.6 1.6 %copy-done.8 = bf16[128,8,1536]{2,1,0:T(8,128)(2,1)} copy-done((bf16[128,8,1536]{2,1,0:T(8,128)(2,1)}, bf16[128,8,1536]{2,1,0:T(8,128)(2,1)S(1)}, u32[]{:S(2)}) %copy-start.8) | copy-done | bytes 3145752
  60.3 0.0 copy-done.4
  60.3 11.8 %filter.1 = bf16[1024,1536]{1,0:T(8,128)(2,1)} custom-call(bf16[1024,1536]{1,0:T(8,128)(2,1)} %bitcast.10, s32[2,1536]{1,0:T(2,128)S(1)} %copy-done.4, f32[1,1536]{1,0:T(1,128)S(1)} %reshape.25.taper_ref, bf16[2,1536,1536]{2,1,0:T(8,128)(2,1)} %filters_ref.1), custom_call_target="tpu_custom_call" | custom-call | tf_op jit(solution)/shard_map/filter/pallas_call | solution.py:158
  72.1 0.0 copy-start.6
  72.1 0.0 copy-start.7
  72.1 6.1 %all-to-all-start.1 = ((bf16[128,8,1536]{2,1,0:T(8,128)(2,1)}), bf16[128,8,1536]{2,1,0:T(8,128)(2,1)S(1)}, u32[]{:S(2)}, u32[]{:S(2)}) async-start(bf16[128,8,1536]{2,1,0:T(8,128)(2,1)} %bitcast.3), calls=%async_computation.1 | async-start | bytes 6291456 | tf_op jit(solution)/shard_map/all_to_all | solution.py:220
  78.2 0.0 copy-done.6
  78.2 0.0 copy-done.7
  78.2 0.4 indices.1
  78.7 0.0 copy-start.2
  78.7 1.0 copy-done.2
  79.6 0.8 fusion.9
  80.4 1.3 sine_multiply_fusion
  81.7 4.7 %tables.1 = (bf16[1536,1536]{1,0:T(8,128)(2,1)S(1)}, bf16[1536,1536]{1,0:T(8,128)(2,1)}) custom-call(f32[48,1536]{1,0:T(8,128)S(1)} %get-tuple-element.14.coarse_cos_ref, f32[48,1536]{1,0:T(8,128)S(1)} %get-tuple-element.13.coarse_sin_ref, f32[32,1536]{1,0:T(8,128)S(1)} %get-tuple-element.16.fine_cos_ref, f32[32,1536]{1,0:T(8,128)S(1)} %get-tuple-element.15.fine_sin_ref), custom_call_target="tpu_custom_call" | custom-call | tf_op jit(solution)/shard_map/tables/pallas_call | solution.py:116
  86.4 0.0 copy-start.1
  86.4 2.2 %copy-done.1 = bf16[1536,1536]{1,0:T(8,128)(2,1)} copy-done((bf16[1536,1536]{1,0:T(8,128)(2,1)}, bf16[1536,1536]{1,0:T(8,128)(2,1)S(1)}, u32[]{:S(2)}) %copy-start.1) | copy-done | bytes 4718616
  88.6 31.5 %all-to-all-done.1 = bf16[128,8,1536]{2,1,0:T(8,128)(2,1)S(1)} async-done(((bf16[128,8,1536]{2,1,0:T(8,128)(2,1)}), bf16[128,8,1536]{2,1,0:T(8,128)(2,1)S(1)}, u32[]{:S(2)}, u32[]{:S(2)}) %all-to-all-start.1) | async-done | bytes 3145760 | tf_op jit(solution)/shard_map/all_to_all | solution.py:220
  120.1 0.0 copy-start.3
  120.1 1.2 copy-done.3
  121.3 12.2 %power.1 = f32[256,1536]{1,0:T(8,128)} custom-call(bf16[1024,1536]{1,0:T(8,128)(2,1)S(1)} %bitcast.6, bf16[512,1024]{1,0:T(8,128)(2,1)S(1)} %copy-done.3, bf16[256,256]{1,0:T(8,128)(2,1)S(1)} %get-tuple-element.10.second_ref, bf16[1536,1536]{1,0:T(8,128)(2,1)} %copy-done.1, bf16[1536,1536]{1,0:T(8,128)(2,1)} %get-tuple-element.12.sin_ref), custom_call_target="tpu_custom_call" | custom-call | tf_op jit(solution)/shard_map/power/pallas_call | solution.py:200
  (2 shorter events, 0.0 us)
Async XLA Ops:
  0.0 1.4 %copy-start = (bf16[256,3072]{1,0:T(8,128)(2,1)S(1)}, bf16[256,3072]{1,0:T(8,128)(2,1)}, u32[]{:S(2)}) copy-start(bf16[256,3072]{1,0:T(8,128)(2,1)} %imag_ref.1) | copy-start | bytes 4718596
  1.4 0.7 copy-start.5
  6.3 10.5 %copy-start.9 = (f32[1536]{0:T(1024)S(1)}, f32[1536]{0:T(1024)}, u32[]{:S(2)}) copy-start(f32[1536]{0:T(1024)} %param.10) | copy-start | bytes 18436
  6.3 54.0 %copy-start.4 = (s32[2,1536]{1,0:T(2,128)S(1)}, s32[2,1536]{1,0:T(2,128)}, u32[]{:S(2)}) copy-start(s32[2,1536]{1,0:T(2,128)} %flags_ref.1) | copy-start | bytes 36868
  6.3 52.3 %all-to-all-start = ((bf16[128,8,1536]{2,1,0:T(8,128)(2,1)}), bf16[128,8,1536]{2,1,0:T(8,128)(2,1)S(1)}, u32[]{:S(2)}, u32[]{:S(2)}) async-start(bf16[128,8,1536]{2,1,0:T(8,128)(2,1)} %bitcast.1), calls=%async_computation | async-start | bytes 6291456 | tf_op jit(solution)/shard_map/all_to_all | solution.py:220
  58.6 1.7 %copy-start.8 = (bf16[128,8,1536]{2,1,0:T(8,128)(2,1)}, bf16[128,8,1536]{2,1,0:T(8,128)(2,1)S(1)}, u32[]{:S(2)}) copy-start(bf16[128,8,1536]{2,1,0:T(8,128)(2,1)S(1)} %all-to-all-done) | copy-start | bytes 9437188
  72.1 6.1 %copy-start.6 = (s32[256,1]{0,1:T(1,128)S(1)}, s32[256,1]{0,1:T(1,128)}, u32[]{:S(2)}) copy-start(s32[256,1]{0,1:T(1,128)} %param.7) | copy-start | bytes 3076
  72.1 6.1 %copy-start.7 = (s32[256,2]{0,1:T(2,128)S(1)}, s32[256,2]{0,1:T(2,128)}, u32[]{:S(2)}) copy-start(s32[256,2]{0,1:T(2,128)} %param.11) | copy-start | bytes 6148
  72.1 47.9 %all-to-all-start.1 = ((bf16[128,8,1536]{2,1,0:T(8,128)(2,1)}), bf16[128,8,1536]{2,1,0:T(8,128)(2,1)S(1)}, u32[]{:S(2)}, u32[]{:S(2)}) async-start(bf16[128,8,1536]{2,1,0:T(8,128)(2,1)} %bitcast.3), calls=%async_computation.1 | async-start | bytes 6291456 | tf_op jit(solution)/shard_map/all_to_all | solution.py:220
  78.7 1.0 copy-start.2
  86.4 2.2 %copy-start.1 = (bf16[1536,1536]{1,0:T(8,128)(2,1)}, bf16[1536,1536]{1,0:T(8,128)(2,1)S(1)}, u32[]{:S(2)}) copy-start(bf16[1536,1536]{1,0:T(8,128)(2,1)S(1)} %get-tuple-element.11.cos_ref) | copy-start | bytes 14155780
  120.1 1.2 copy-start.3

commit v2 on v1

v2 whole, which is shorter than its diff:
```python
import math

import jax
import jax.numpy as jnp
from jax import lax
from jax.experimental import pallas as pl
from jax.experimental.pallas import tpu as pltpu
from jax.sharding import PartitionSpec as P

BF16 = jnp.bfloat16
F32 = jnp.float32
SLOTS = 2
PARTS = 2
TILE = 8


def iota(shape, axis):
    return lax.broadcasted_iota(jnp.int32, shape, axis)


def row_of_slot(labels_row):
    count = labels_row.shape[1]
    across = jnp.broadcast_to(labels_row.astype(F32), (count, count))
    down = across.T
    earlier = iota((count, count), 0) < iota((count, count), 1)
    slot = jnp.sum(jnp.where((across == down) & earlier, 1.0, 0.0), axis=0, keepdims=True)
    slot = slot.astype(jnp.int32)
    return (labels_row >> 1) * TILE + (labels_row & 1) * (PARTS * SLOTS) + slot


def pack_kernel(labels_ref, rows_hbm, out_hbm, rows_ref, select_ref, out_ref, in_sems, out_sems):
    rows, width = out_ref.shape
    count = rows_ref.shape[0] // PARTS
    steps = out_sems.shape[0]
    step = width // steps
    columns = [pl.ds(j * step, step) for j in range(steps)]
    loads = [
        [
            pltpu.make_async_copy(
                rows_hbm.at[:, pl.ds(part * width + j * step, step)],
                rows_ref.at[pl.ds(part * count, count), at],
                in_sems.at[part, j],
            )
            for part in range(PARTS)
        ]
        for j, at in enumerate(columns)
    ]
    stores = [
        pltpu.make_async_copy(out_ref.at[:, at], out_hbm.at[:, at], out_sems.at[j])
        for j, at in enumerate(columns)
    ]
    for pair in loads:
        for load in pair:
            load.start()
    place = row_of_slot(labels_ref[...])
    index = iota((rows, count), 0)
    select_ref[:, :count] = jnp.where(index == place, 1.0, 0.0).astype(BF16)
    select_ref[:, count:] = jnp.where(index == place + SLOTS, 1.0, 0.0).astype(BF16)
    for j, at in enumerate(columns):
        for load in loads[j]:
            load.wait()
        stacked = rows_ref[:, at]
        out_ref[:, at] = jnp.dot(
            select_ref[...], stacked, preferred_element_type=F32
        ).astype(BF16)
        stores[j].start()
    for store in stores:
        store.wait()


def pack(labels_row, visibilities, rows, width, step):
    count = visibilities.shape[0]
    steps = width // step
    anywhere = pl.BlockSpec(memory_space=pl.ANY)
    return pl.pallas_call(
        pack_kernel,
        in_specs=[pl.BlockSpec(memory_space=pltpu.VMEM), anywhere],
        out_specs=anywhere,
        out_shape=pltpu.HBM((rows, width), BF16),
        scratch_shapes=[
            pltpu.VMEM((PARTS * count, width), BF16),
            pltpu.VMEM((rows, PARTS * count), BF16),
            pltpu.VMEM((rows, width), BF16),
            pltpu.SemaphoreType.DMA((PARTS, steps)),
            pltpu.SemaphoreType.DMA((steps,)),
        ],
        compiler_params=pltpu.CompilerParams(vmem_limit_bytes=24 << 20),
        name="pack",
    )(labels_row, visibilities)


def index_kernel(labels_ref, pairs_ref, source_ref, second_ref):
    count = labels_ref.shape[1]
    place = row_of_slot(labels_ref[...])
    local = (pairs_ref[...] & (count - 1)).astype(F32)
    first = jnp.broadcast_to(local[0:1], (count, count))
    other = jnp.broadcast_to(local[1:2], (count, count))
    first_down = first.T.astype(jnp.int32)
    lane = iota((count, count), 1)
    source = jnp.sum(
        jnp.where(first_down == lane, place.astype(F32), 0.0), axis=1, keepdims=True
    ).astype(jnp.int32)
    source_ref[...] = source
    second_ref[...] = jnp.where(other.T == first, 1.0, 0.0).astype(BF16)


def indices(labels_row, pairs_rows):
    count = labels_row.shape[1]
    return pl.pallas_call(
        index_kernel,
        out_shape=(
            jax.ShapeDtypeStruct((count, 1), jnp.int32),
            jax.ShapeDtypeStruct((count, count), BF16),
        ),
        compiler_params=pltpu.CompilerParams(vmem_limit_bytes=24 << 20),
        name="indices",
    )(labels_row, pairs_rows)


def table_kernel(coarse_cos_ref, coarse_sin_ref, fine_cos_ref, fine_sin_ref, taper_ref, out_ref):
    fine, half = fine_cos_ref.shape
    scale = 1.0 / math.sqrt(PARTS * half)
    fine_cos, fine_sin = fine_cos_ref[...], fine_sin_ref[...]
    start = iota((fine, half), 1) == 0
    turn = jnp.where(iota((fine, half), 0) & 1 == 0, scale, -scale)
    for i in range(out_ref.shape[0] // fine):
        coarse_cos, coarse_sin = coarse_cos_ref[i : i + 1, :], coarse_sin_ref[i : i + 1, :]
        at = pl.ds(i * fine, fine)
        taper = taper_ref[at, :]
        cosines = (coarse_cos * fine_cos - coarse_sin * fine_sin).astype(BF16).astype(F32)
        sines = coarse_sin * fine_cos + coarse_cos * fine_sin
        sines = jnp.where(start, turn, sines).astype(BF16).astype(F32)
        out_ref[at, :half] = (cosines * taper).astype(BF16)
        out_ref[at, half:] = (sines * taper).astype(BF16)


def tapered_tables(width, taper_column, fine):
    half = width // 2

    def angles(rows, spacing):
        n = jnp.arange(rows, dtype=jnp.int32) * spacing
        phase = n[:, None] * jnp.arange(half, dtype=jnp.int32)[None, :] % width
        return phase.astype(F32) * (2.0 * math.pi / width)

    coarse, small = angles(width // fine, fine), angles(fine, 1)
    scale = 1.0 / math.sqrt(width)
    return pl.pallas_call(
        table_kernel,
        out_shape=jax.ShapeDtypeStruct((width, width), BF16),
        compiler_params=pltpu.CompilerParams(vmem_limit_bytes=24 << 20),
        name="tables",
    )(jnp.cos(coarse) * scale, jnp.sin(coarse) * scale, jnp.cos(small), jnp.sin(small), taper_column)


def combine_kernel(filters_ref, keep_ref, table_ref, out_ref):
    which = pl.program_id(0)
    keep = jnp.where(which == 0, keep_ref[:, 0:1], keep_ref[:, 1:2])
    product = jnp.dot(filters_ref[0], table_ref[...], preferred_element_type=F32)
    out_ref[0] = (product * keep).astype(BF16)


def combine(filters, keep_columns, table, step):
    classes, width, _ = filters.shape
    block = pl.BlockSpec((1, step, width), lambda w, i: (w, i, 0))
    return pl.pallas_call(
        combine_kernel,
        grid=(classes, width // step),
        in_specs=[
            block,
            pl.BlockSpec((step, classes), lambda w, i: (i, 0)),
            pl.BlockSpec((width, width), lambda w, i: (0, 0), pipeline_mode=pl.Buffered(1)),
        ],
        out_specs=block,
        out_shape=pltpu.HBM((classes, width, width), BF16),
        compiler_params=pltpu.CompilerParams(vmem_limit_bytes=24 << 20),
        name="combine",
    )(filters, keep_columns, table)


def filter_kernel(arrived_ref, matrix_hbm, out_hbm, split_ref, matrix_ref, out_ref, in_sems, out_sems):
    rows, width = arrived_ref.shape
    steps = in_sems.shape[0]
    step = width // steps
    half = TILE // 2
    pairs = rows // (2 * TILE)
    columns = [pl.ds(j * step, step) for j in range(steps)]
    loads = [
        pltpu.make_async_copy(matrix_hbm.at[:, :, at], matrix_ref.at[:, :, at], in_sems.at[j])
        for j, at in enumerate(columns)
    ]
    stores = [
        pltpu.make_async_copy(out_ref.at[:, at], out_hbm.at[:, at], out_sems.at[j])
        for j, at in enumerate(columns)
    ]
    for load in loads:
        load.start()
    low = iota((1, TILE, 1), 1) < half
    arrived = arrived_ref[...].astype(F32).reshape(pairs, 2, TILE, width)
    even, odd = arrived[:, 0], arrived[:, 1]
    first = jnp.where(low, even, pltpu.roll(odd, half, 1))
    second = jnp.where(low, pltpu.roll(even, half, 1), odd)
    split_ref[0] = first.reshape(rows // 2, width).astype(BF16)
    split_ref[1] = second.reshape(rows // 2, width).astype(BF16)
    for j, at in enumerate(columns):
        loads[j].wait()
        done = [
            jnp.dot(split_ref[w], matrix_ref[w, :, at], preferred_element_type=F32)
            .reshape(pairs, TILE, step)
            for w in range(2)
        ]
        even = jnp.where(low, done[0], pltpu.roll(done[1], half, 1))
        odd = jnp.where(low, pltpu.roll(done[0], half, 1), done[1])
        both = jnp.concatenate([even[:, None], odd[:, None]], axis=1)
        out_ref[:, at] = both.reshape(rows, step).astype(BF16)
        stores[j].start()
    for store in stores:
        store.wait()


def filter_rows(arrived, matrices, step):
    rows, width = arrived.shape
    anywhere = pl.BlockSpec(memory_space=pl.ANY)
    return pl.pallas_call(
        filter_kernel,
        in_specs=[pl.BlockSpec(memory_space=pltpu.VMEM), anywhere],
        out_specs=anywhere,
        out_shape=pltpu.HBM((rows, width), BF16),
        scratch_shapes=[
            pltpu.VMEM((2, rows // 2, width), BF16),
            pltpu.VMEM((2, width, width), BF16),
            pltpu.VMEM((rows, width), BF16),
            pltpu.SemaphoreType.DMA((width // step,)),
            pltpu.SemaphoreType.DMA((width // step,)),
        ],
        compiler_params=pltpu.CompilerParams(vmem_limit_bytes=40 << 20),
        name="filter",
    )(arrived, matrices)


def power_kernel(returned_ref, source_ref, second_ref, out_ref):
    count = second_ref.shape[0]
    rows, width = returned_ref.shape
    half, lanes, step = width // 2, 128, 256
    second = second_ref[...]
    index = iota((count, rows), 1)
    fetch = jnp.concatenate(
        [
            jnp.where(index == source_ref[...] + part * SLOTS, 1.0, 0.0).astype(BF16)
            for part in range(PARTS)
        ],
        axis=0,
    )
    mirror = (lanes - iota((count, lanes), 1)) & (lanes - 1)
    start = iota((count, step), 1) == 0
    mirrored = []
    for j in range(half // step):
        at = pl.ds(j * step, step)
        cos_sum = jnp.dot(fetch, returned_ref[:, at], preferred_element_type=F32)
        sin_sum = jnp.dot(
            fetch, returned_ref[:, pl.ds(half + j * step, step)], preferred_element_type=F32
        )
        cos_real, cos_imag = cos_sum[:count], cos_sum[count:]
        sin_real, sin_imag = sin_sum[:count], sin_sum[count:]
        far_real, far_imag = cos_real, cos_imag
        if j == 0:
            far_real = jnp.where(start, sin_real, cos_real)
            far_imag = jnp.where(start, sin_imag, cos_imag)
            sin_real = jnp.where(start, 0.0, sin_real)
            sin_imag = jnp.where(start, 0.0, sin_imag)
        spectra = jnp.concatenate(
            [cos_real + sin_imag, cos_imag - sin_real, far_real - sin_imag, far_imag + sin_real],
            axis=1,
        ).astype(BF16)
        other = jnp.dot(second, spectra, preferred_element_type=F32)
        product = spectra.astype(F32) * other
        out_ref[:, at] = product[:, :step] + product[:, step : 2 * step]
        far = product[:, 2 * step : 3 * step] + product[:, 3 * step :]
        for block in range(step // lanes):
            part = far[:, block * lanes : (block + 1) * lanes]
            mirrored.append(jnp.take_along_axis(part, mirror, axis=1))
    blocks = half // lanes
    first = iota((count, lanes), 1) == 0
    for b in range(blocks):
        out_ref[:, pl.ds(half + b * lanes, lanes)] = jnp.where(
            first, mirrored[(blocks - b) % blocks], mirrored[blocks - 1 - b]
        )


def cross_power(returned, source, second):
    width = returned.shape[1]
    count = second.shape[0]
    return pl.pallas_call(
        power_kernel,
        out_shape=jax.ShapeDtypeStruct((count, width), F32),
        compiler_params=pltpu.CompilerParams(vmem_limit_bytes=24 << 20),
        name="power",
    )(returned, source, second)


def exchange(packed, peers):
    rows, width = packed.shape
    moved = lax.all_to_all(
        packed.reshape(peers, rows // peers, width),
        ("tm", "cls"),
        split_axis=0,
        concat_axis=0,
        tiled=True,
    )
    return moved.reshape(rows, width)


def local(visibilities, row_class, filters, flags, taper, pairs):
    count = visibilities.shape[0]
    classes, width = filters.shape[0], filters.shape[1]
    peers = lax.axis_size(("tm", "cls"))
    rows = peers * TILE
    assert classes == 2 and count & (count - 1) == 0
    labels_row = row_class.reshape(1, count)
    in_hbm = lambda x: pltpu.with_memory_space_constraint(x, pltpu.HBM)
    packed = pack(in_hbm(labels_row), in_hbm(visibilities), rows, width, 512)
    arrived = exchange(packed, peers)
    source, second = indices(labels_row, pairs.T)
    table = tapered_tables(width, taper.reshape(width, 1), 32)
    matrices = combine(in_hbm(filters), (1 - flags).astype(F32).T, table, 512)
    summed = filter_rows(arrived, in_hbm(matrices), 256)
    returned = exchange(summed, peers)
    return cross_power(returned, source, second)


def solution(mesh):
    across = ("tm", "cls")
    placed = (
        P(across, None),
        P(across, None),
        P(across, None, None),
        P(across, None),
        P(),
        P(across, None),
    )
    return jax.shard_map(
        local, mesh=mesh, in_specs=placed, out_specs=P(across, None), check_vma=False
    )
```

time: 134 us -> 118 us (0.88)
  waiting for transfers between devices: 73.3 us -> 58.2 us
  Pallas kernels: 33.3 us -> 38 us
  local copies, waits for them, and re-layouts: 8.12 us -> 3.5 us
    all_to_all x2, waiting for transfers between devices: 73.3 us -> 58.2 us  [exchange(): lax.all_to_all(packed.reshape(peers, rows // peers, width), ('tm', 'cls')...]
    unnamed x20 -> x12, local copies, waits for them, and re-layouts: 8.11 us -> 1.16 us
    pallas_call x5 -> x6, Pallas kernels: 33.3 us -> 38 us  [the longest x1 18.4 us: combine(): pl.pallas_call(combine_kernel, grid=(classes, width // step), in_specs=[b...]
  transfers between devices with their start and end apart: 2 -> 2, of which waited for: 2 -> 2; matrix products, arithmetic and copies ran while one was open for 2% -> 3% of each run, Pallas kernels for 4% -> 18%
where the time goes in v2:
time: 118 us
  waiting for transfers between devices  58.2 us (49%)
  Pallas kernels  38 us (32%)
  starting transfers between devices  16.6 us (14%)
  local copies, waits for them, and re-layouts  3.5 us (3%)
    all_to_all x2, waiting for transfers between devices, exchange(): lax.all_to_all(packed.reshape(peers, rows // peers, width), ('tm', 'cls')...  58.2 us
    pallas_call x1, Pallas kernels, combine(): pl.pallas_call(combine_kernel, grid=(classes, width // step), in_specs=[b...  18.4 us
    all_to_all x2, starting transfers between devices, exchange(): lax.all_to_all(packed.reshape(peers, rows // peers, width), ('tm', 'cls')...  16.6 us
    pallas_call x1, Pallas kernels, filter_rows(): pl.pallas_call(filter_kernel, in_specs=[pl.BlockSpec(memory_space=pltpu.V...  8.4 us
    pallas_call x1, Pallas kernels, pack(): pl.pallas_call(pack_kernel, in_specs=[pl.BlockSpec(memory_space=pltpu.VME...  4.97 us
    pallas_call x1, Pallas kernels, cross_power(): pl.pallas_call(power_kernel, out_shape=jax.ShapeDtypeStruct((count, width...  3.85 us
  transfers between devices with their start and end apart: 2, of which 2 were waited for; matrix products, arithmetic and copies ran while one was open for 3% of the time, Pallas kernels for 18%

profile of v2, /device:TPU:4, one launch (start us, length us, event | category | flops | bytes accessed | tf_op | source)
XLA Modules:
  0.0 117.6 jit_solution(16567954172503419598)
XLA Ops:
  0.0 5.0 %pack.1 = bf16[1024,1536]{1,0:T(8,128)(2,1)} custom-call(s32[1,256]{1,0:T(1,128)} %bitcast.10, bf16[256,3072]{1,0:T(8,128)(2,1)} %rows_hbm.1), custom_call_target="tpu_custom_call" | custom-call | tf_op jit(solution)/shard_map/pack/pallas_call | solution.py:75
  5.0 0.0 copy-start.5
  5.0 0.0 copy-start.4
  5.0 10.5 %all-to-all-start = ((bf16[128,8,1536]{2,1,0:T(8,128)(2,1)}), bf16[128,8,1536]{2,1,0:T(8,128)(2,1)S(1)}, u32[]{:S(2)}, u32[]{:S(2)}) async-start(bf16[128,8,1536]{2,1,0:T(8,128)(2,1)} %bitcast.13), calls=%async_computation | async-start | bytes 6291456 | tf_op jit(solution)/shard_map/all_to_all | solution.py:302
  15.5 0.0 copy-done.5
  15.5 1.2 reshape.28.taper_ref
  16.7 0.0 copy-done.4
  16.7 1.2 %copy.12 = f32[2,1536]{0,1:T(8,128)} copy(f32[2,1536]{1,0:T(2,128)S(1)} %subtract_convert_fusion) | data formatting | bytes 24576 | tf_op jit(solution)/shard_map/convert_element_type | solution.py:324
  17.9 0.4 fusion.9
  18.3 0.0 copy-start
  18.3 0.7 sine_multiply_fusion
  19.0 0.0 copy-start.1
  19.0 1.1 copy-done.1
  20.1 2.2 %tables.1.table_ref = bf16[1536,1536]{1,0:T(8,128)(2,1)S(1)} custom-call(f32[48,768]{1,0:T(8,128)S(1)} %get-tuple-element.10.coarse_cos_ref, f32[48,768]{1,0:T(8,128)S(1)} %get-tuple-element.9.coarse_sin_ref, f32[32,768]{1,0:T(8,128)S(1)} %get-tuple-element.12.fine_cos_ref, f32[32,768]{1,0:T(8,128)S(1)} %get-tuple-element.11.fine_sin_ref, ...), custom_call_target="tpu_custom_call" | custom-call | tf_op jit(solution)/shard_map/tables/pallas_call | solution.py:147
  22.3 0.0 copy-done
  22.3 18.4 %combine.1.matrix_hbm = bf16[2,1536,1536]{2,1,0:T(8,128)(2,1)} custom-call(bf16[2,1536,1536]{2,1,0:T(8,128)(2,1)} %filters_ref.1, f32[1536,2]{1,0:T(8,128)S(1)} %bitcast.9, bf16[1536,1536]{1,0:T(8,128)(2,1)S(1)} %tables.1.table_ref), custom_call_target="tpu_custom_call" | custom-call | tf_op jit(solution)/shard_map/combine/pallas_call | solution.py:165
  40.7 16.7 %all-to-all-done = bf16[128,8,1536]{2,1,0:T(8,128)(2,1)S(1)} async-done(((bf16[128,8,1536]{2,1,0:T(8,128)(2,1)}), bf16[128,8,1536]{2,1,0:T(8,128)(2,1)S(1)}, u32[]{:S(2)}, u32[]{:S(2)}) %all-to-all-start) | async-done | bytes 3145760 | tf_op jit(solution)/shard_map/all_to_all | solution.py:302
  57.4 8.4 %filter.1 = bf16[1024,1536]{1,0:T(8,128)(2,1)} custom-call(bf16[1024,1536]{1,0:T(8,128)(2,1)S(1)} %bitcast.8, bf16[2,1536,1536]{2,1,0:T(8,128)(2,1)} %combine.1.matrix_hbm), custom_call_target="tpu_custom_call" | custom-call | tf_op jit(solution)/shard_map/filter/pallas_call | solution.py:223
  65.8 0.0 copy-start.2
  65.8 0.0 copy-start.3
  65.8 6.1 %all-to-all-start.1 = ((bf16[128,8,1536]{2,1,0:T(8,128)(2,1)}), bf16[128,8,1536]{2,1,0:T(8,128)(2,1)S(1)}, u32[]{:S(2)}, u32[]{:S(2)}) async-start(bf16[128,8,1536]{2,1,0:T(8,128)(2,1)} %bitcast.14), calls=%async_computation.1 | async-start | bytes 6291456 | tf_op jit(solution)/shard_map/all_to_all | solution.py:302
  71.9 0.0 copy-done.2
  71.9 0.0 copy-done.3
  71.9 0.3 indices.1
  72.2 41.5 %all-to-all-done.1 = bf16[128,8,1536]{2,1,0:T(8,128)(2,1)S(1)} async-done(((bf16[128,8,1536]{2,1,0:T(8,128)(2,1)}), bf16[128,8,1536]{2,1,0:T(8,128)(2,1)S(1)}, u32[]{:S(2)}, u32[]{:S(2)}) %all-to-all-start.1) | async-done | bytes 3145760 | tf_op jit(solution)/shard_map/all_to_all | solution.py:302
  113.7 3.9 %power.1 = f32[256,1536]{1,0:T(8,128)} custom-call(bf16[1024,1536]{1,0:T(8,128)(2,1)S(1)} %bitcast.7, s32[256,1]{1,0:T(8,128)S(1)} %get-tuple-element.7.source_ref, bf16[256,256]{1,0:T(8,128)(2,1)S(1)} %get-tuple-element.8.second_ref), custom_call_target="tpu_custom_call" | custom-call | tf_op jit(solution)/shard_map/power/pallas_call | solution.py:292
  (2 shorter events, 0.0 us)
Async XLA Ops:
  5.0 10.5 %copy-start.5 = (f32[1536]{0:T(1024)S(1)}, f32[1536]{0:T(1024)}, u32[]{:S(2)}) copy-start(f32[1536]{0:T(1024)} %param.10) | copy-start | bytes 18436
  5.0 11.7 %copy-start.4 = (s32[2,1536]{1,0:T(2,128)S(1)}, s32[2,1536]{1,0:T(2,128)}, u32[]{:S(2)}) copy-start(s32[2,1536]{1,0:T(2,128)} %param.9) | copy-start | bytes 36868
  5.0 52.4 %all-to-all-start = ((bf16[128,8,1536]{2,1,0:T(8,128)(2,1)}), bf16[128,8,1536]{2,1,0:T(8,128)(2,1)S(1)}, u32[]{:S(2)}, u32[]{:S(2)}) async-start(bf16[128,8,1536]{2,1,0:T(8,128)(2,1)} %bitcast.13), calls=%async_computation | async-start | bytes 6291456 | tf_op jit(solution)/shard_map/all_to_all | solution.py:302
  18.3 4.0 %copy-start = (f32[2,1536]{0,1:T(8,128)S(1)}, f32[2,1536]{0,1:T(8,128)}, u32[]{:S(2)}) copy-start(f32[2,1536]{0,1:T(8,128)} %copy.12) | copy-start | bytes 36868
  19.0 1.1 copy-start.1
  65.8 6.1 %copy-start.2 = (s32[256,1]{0,1:T(1,128)S(1)}, s32[256,1]{0,1:T(1,128)}, u32[]{:S(2)}) copy-start(s32[256,1]{0,1:T(1,128)} %param.7) | copy-start | bytes 3076
  65.8 6.1 %copy-start.3 = (s32[256,2]{0,1:T(2,128)S(1)}, s32[256,2]{0,1:T(2,128)}, u32[]{:S(2)}) copy-start(s32[256,2]{0,1:T(2,128)} %param.11) | copy-start | bytes 6148
  65.8 47.9 %all-to-all-start.1 = ((bf16[128,8,1536]{2,1,0:T(8,128)(2,1)}), bf16[128,8,1536]{2,1,0:T(8,128)(2,1)S(1)}, u32[]{:S(2)}, u32[]{:S(2)}) async-start(bf16[128,8,1536]{2,1,0:T(8,128)(2,1)} %bitcast.14), calls=%async_computation.1 | async-start | bytes 6291456 | tf_op jit(solution)/shard_map/all_to_all | solution.py:302

commit v3 on v2

v3 whole, which is shorter than its diff:
```python
import functools
import math

import jax
import jax.numpy as jnp
from jax import lax
from jax.experimental import pallas as pl
from jax.experimental.pallas import tpu as pltpu
from jax.sharding import PartitionSpec as P

BF16 = jnp.bfloat16
F32 = jnp.float32
SLOTS = 2
PARTS = 2
TILE = 8


def iota(shape, axis):
    return lax.broadcasted_iota(jnp.int32, shape, axis)


def split_width(width, shares):
    unit = width // sum(shares)
    return tuple(share * unit for share in shares)


def slot_of_row(labels_row):
    count = labels_row.shape[1]
    across = jnp.broadcast_to(labels_row.astype(F32), (count, count))
    down = across.T
    earlier = iota((count, count), 0) < iota((count, count), 1)
    place = jnp.sum(jnp.where((across == down) & earlier, 1.0, 0.0), axis=0, keepdims=True)
    return labels_row * SLOTS + place.astype(jnp.int32)


def weave(first, second):
    rows, width = first.shape
    groups = (rows // TILE, TILE, width)
    first, second = first.reshape(groups), second.reshape(groups)
    low = iota((1, TILE, 1), 1) < TILE // 2
    even = jnp.where(low, first, pltpu.roll(second, TILE // 2, 1))
    odd = jnp.where(low, pltpu.roll(first, TILE // 2, 1), second)
    return jnp.concatenate([even[:, None], odd[:, None]], axis=1).reshape(2 * rows, width)


def pieces(sizes):
    starts = [sum(sizes[:i]) for i in range(len(sizes))]
    return [pl.ds(start, size) for start, size in zip(starts, sizes)]


def pack_kernel(sizes, labels_ref, rows_hbm, out_hbm, rows_ref, select_ref, out_ref, in_sems, out_sems):
    columns = pieces(sizes)
    width = out_ref.shape[1]
    loads = [
        [
            pltpu.make_async_copy(
                rows_hbm.at[:, pl.ds(part * width + at.start, at.size)],
                rows_ref.at[part, :, at],
                in_sems.at[part, j],
            )
            for part in range(PARTS)
        ]
        for j, at in enumerate(columns)
    ]
    stores = [
        pltpu.make_async_copy(out_ref.at[:, at], out_hbm.at[:, at], out_sems.at[j])
        for j, at in enumerate(columns)
    ]
    for pair in loads:
        for load in pair:
            load.start()
    select_ref[...] = jnp.where(
        iota(select_ref.shape, 0) == slot_of_row(labels_ref[...]), 1.0, 0.0
    ).astype(BF16)
    for j, at in enumerate(columns):
        for load in loads[j]:
            load.wait()
        parts = [
            jnp.dot(select_ref[...], rows_ref[part, :, at], preferred_element_type=F32)
            for part in range(PARTS)
        ]
        out_ref[:, at] = weave(*parts).astype(BF16)
        stores[j].start()
    for store in stores:
        store.wait()


def pack(labels_row, visibilities, rows, sizes):
    count, width = visibilities.shape[0], sum(sizes)
    anywhere = pl.BlockSpec(memory_space=pl.ANY)
    return pl.pallas_call(
        functools.partial(pack_kernel, sizes),
        in_specs=[pl.BlockSpec(memory_space=pltpu.VMEM), anywhere],
        out_specs=anywhere,
        out_shape=pltpu.HBM((rows, width), BF16),
        scratch_shapes=[
            pltpu.VMEM((PARTS, count, width), BF16),
            pltpu.VMEM((rows // PARTS, count), BF16),
            pltpu.VMEM((rows, width), BF16),
            pltpu.SemaphoreType.DMA((PARTS, len(sizes))),
            pltpu.SemaphoreType.DMA((len(sizes),)),
        ],
        compiler_params=pltpu.CompilerParams(vmem_limit_bytes=24 << 20),
        name="pack",
    )(labels_row, visibilities)


def index_kernel(labels_ref, pairs_ref, source_ref, second_ref):
    count = labels_ref.shape[1]
    slots = slot_of_row(labels_ref[...])
    each = TILE // PARTS
    place = slots // each * TILE + slots % each
    local = (pairs_ref[...] & (count - 1)).astype(F32)
    first = jnp.broadcast_to(local[0:1], (count, count))
    other = jnp.broadcast_to(local[1:2], (count, count))
    first_down = first.T.astype(jnp.int32)
    lane = iota((count, count), 1)
    source = jnp.sum(
        jnp.where(first_down == lane, place.astype(F32), 0.0), axis=1, keepdims=True
    ).astype(jnp.int32)
    source_ref[...] = source
    second_ref[...] = jnp.where(other.T == first, 1.0, 0.0).astype(BF16)


def indices(labels_row, pairs_rows):
    count = labels_row.shape[1]
    return pl.pallas_call(
        index_kernel,
        out_shape=(
            jax.ShapeDtypeStruct((count, 1), jnp.int32),
            jax.ShapeDtypeStruct((count, count), BF16),
        ),
        compiler_params=pltpu.CompilerParams(vmem_limit_bytes=24 << 20),
        name="indices",
    )(labels_row, pairs_rows)


def table_kernel(coarse_cos_ref, coarse_sin_ref, fine_cos_ref, fine_sin_ref, taper_ref, out_ref):
    fine, half = fine_cos_ref.shape
    scale = 1.0 / math.sqrt(PARTS * half)
    fine_cos, fine_sin = fine_cos_ref[...], fine_sin_ref[...]
    start = iota((fine, half), 1) == 0
    turn = jnp.where(iota((fine, half), 0) & 1 == 0, scale, -scale)
    for i in range(out_ref.shape[0] // fine):
        coarse_cos, coarse_sin = coarse_cos_ref[i : i + 1, :], coarse_sin_ref[i : i + 1, :]
        at = pl.ds(i * fine, fine)
        taper = taper_ref[at, :]
        cosines = (coarse_cos * fine_cos - coarse_sin * fine_sin).astype(BF16).astype(F32)
        sines = coarse_sin * fine_cos + coarse_cos * fine_sin
        sines = jnp.where(start, turn, sines).astype(BF16).astype(F32)
        out_ref[at, :half] = (cosines * taper).astype(BF16)
        out_ref[at, half:] = (sines * taper).astype(BF16)


def tapered_tables(width, taper_column, fine):
    half = width // 2

    def angles(rows, spacing):
        n = jnp.arange(rows, dtype=jnp.int32) * spacing
        phase = n[:, None] * jnp.arange(half, dtype=jnp.int32)[None, :] % width
        return phase.astype(F32) * (2.0 * math.pi / width)

    coarse, small = angles(width // fine, fine), angles(fine, 1)
    scale = 1.0 / math.sqrt(width)
    return pl.pallas_call(
        table_kernel,
        out_shape=jax.ShapeDtypeStruct((width, width), BF16),
        compiler_params=pltpu.CompilerParams(vmem_limit_bytes=24 << 20),
        name="tables",
    )(jnp.cos(coarse) * scale, jnp.sin(coarse) * scale, jnp.cos(small), jnp.sin(small), taper_column)


def combine_kernel(filters_ref, keep_ref, table_ref, out_ref):
    which = pl.program_id(0)
    keep = jnp.where(which == 0, keep_ref[:, 0:1], keep_ref[:, 1:2])
    product = jnp.dot(filters_ref[0], table_ref[...], preferred_element_type=F32)
    out_ref[0] = (product * keep).astype(BF16)


def combine(filters, keep_columns, table, step):
    classes, width, _ = filters.shape
    block = pl.BlockSpec((1, step, width), lambda w, i: (w, i, 0))
    return pl.pallas_call(
        combine_kernel,
        grid=(classes, width // step),
        in_specs=[
            block,
            pl.BlockSpec((step, classes), lambda w, i: (i, 0)),
            pl.BlockSpec((width, width), lambda w, i: (0, 0), pipeline_mode=pl.Buffered(1)),
        ],
        out_specs=block,
        out_shape=pltpu.HBM((classes, width, width), BF16),
        compiler_params=pltpu.CompilerParams(vmem_limit_bytes=24 << 20),
        name="combine",
    )(filters, keep_columns, table)


def filter_kernel(sizes, step, arrived_ref, matrix_hbm, out_hbm, split_ref, matrix_ref, out_ref, in_sems, out_sems):
    rows, width = arrived_ref.shape
    columns = pieces(sizes)
    loads = [
        pltpu.make_async_copy(matrix_hbm.at[:, :, at], matrix_ref.at[:, :, at], in_sems.at[j])
        for j, at in enumerate(columns)
    ]
    own = iota((1, TILE, 1), 1) & SLOTS == 0
    loads[0].start()
    groups = len(loads) - 1
    count = rows // (2 * groups)
    for g in range(groups):
        arrived = arrived_ref[pl.ds(2 * g * count, 2 * count), :].astype(F32)
        arrived = arrived.reshape(count // TILE, 2, TILE, width)
        even, odd = arrived[:, 0], arrived[:, 1]
        first = jnp.where(own, even, pltpu.roll(odd, SLOTS, 1))
        second = jnp.where(own, pltpu.roll(even, TILE - SLOTS, 1), odd)
        split_ref[0, pl.ds(g * count, count), :] = first.reshape(count, width).astype(BF16)
        split_ref[1, pl.ds(g * count, count), :] = second.reshape(count, width).astype(BF16)
        loads[g + 1].start()
    stores = []
    for load, piece in zip(loads, columns):
        load.wait()
        for start in range(piece.start, piece.start + piece.size, step):
            at = pl.ds(start, step)
            done = [
                jnp.dot(split_ref[w], matrix_ref[w, :, at], preferred_element_type=F32)
                .reshape(rows // (2 * TILE), TILE, step)
                for w in range(2)
            ]
            even = jnp.where(own, done[0], pltpu.roll(done[1], SLOTS, 1))
            odd = jnp.where(own, pltpu.roll(done[0], TILE - SLOTS, 1), done[1])
            both = jnp.concatenate([even[:, None], odd[:, None]], axis=1)
            out_ref[:, at] = both.reshape(rows, step).astype(BF16)
            store = pltpu.make_async_copy(
                out_ref.at[:, at], out_hbm.at[:, at], out_sems.at[len(stores)]
            )
            store.start()
            stores.append(store)
    for store in stores:
        store.wait()


def filter_rows(arrived, matrices, sizes, step):
    rows, width = arrived.shape
    anywhere = pl.BlockSpec(memory_space=pl.ANY)
    return pl.pallas_call(
        functools.partial(filter_kernel, sizes, step),
        in_specs=[pl.BlockSpec(memory_space=pltpu.VMEM), anywhere],
        out_specs=anywhere,
        out_shape=pltpu.HBM((rows, width), BF16),
        scratch_shapes=[
            pltpu.VMEM((2, rows // 2, width), BF16),
            pltpu.VMEM((2, width, width), BF16),
            pltpu.VMEM((rows, width), BF16),
            pltpu.SemaphoreType.DMA((len(sizes),)),
            pltpu.SemaphoreType.DMA((width // step,)),
        ],
        compiler_params=pltpu.CompilerParams(vmem_limit_bytes=40 << 20),
        name="filter",
    )(arrived, matrices)


def power_kernel(returned_ref, source_ref, second_ref, out_hbm, out_ref, sems):
    count = second_ref.shape[0]
    rows, width = returned_ref.shape
    half, lanes, step = width // 2, 128, 256
    second = second_ref[...]
    index = iota((count, rows), 1)
    fetch = jnp.concatenate(
        [
            jnp.where(index == source_ref[...] + part * (TILE // PARTS), 1.0, 0.0).astype(BF16)
            for part in range(PARTS)
        ],
        axis=0,
    )
    mirror = (lanes - iota((count, lanes), 1)) & (lanes - 1)
    start = iota((count, step), 1) == 0
    edge = iota((count, lanes), 1) == 0
    blocks = half // lanes
    stores = []

    def store(at):
        copy = pltpu.make_async_copy(out_ref.at[:, at], out_hbm.at[:, at], sems.at[len(stores)])
        copy.start()
        stores.append(copy)

    def spectra(sums, j):
        cos_real, cos_imag, sin_real, sin_imag = sums
        far_real, far_imag = cos_real, cos_imag
        if j == 0:
            far_real = jnp.where(start, sin_real, cos_real)
            far_imag = jnp.where(start, sin_imag, cos_imag)
            sin_real = jnp.where(start, 0.0, sin_real)
            sin_imag = jnp.where(start, 0.0, sin_imag)
        return (
            (cos_real + sin_imag, cos_imag - sin_real),
            (far_real - sin_imag, far_imag + sin_real),
        )

    mirrored = []
    waiting = list(range(blocks))
    for j in range(half // step):
        at = pl.ds(j * step, step)
        far_at = pl.ds(half + j * step, step)
        cos_sum = jnp.dot(fetch, returned_ref[:, at], preferred_element_type=F32)
        sin_sum = jnp.dot(fetch, returned_ref[:, far_at], preferred_element_type=F32)
        sums = [cos_sum[:count], cos_sum[count:], sin_sum[:count], sin_sum[count:]]
        others = jnp.dot(
            second, jnp.concatenate(sums, axis=1).astype(BF16), preferred_element_type=F32
        )
        others = [others[:, i * step : (i + 1) * step] for i in range(2 * PARTS)]
        near, far = [
            one[0] * two[0] + one[1] * two[1]
            for one, two in zip(spectra(sums, j), spectra(others, j))
        ]
        out_ref[:, at] = near
        store(at)
        for block in range(step // lanes):
            part = far[:, block * lanes : (block + 1) * lanes]
            mirrored.append(jnp.take_along_axis(part, mirror, axis=1))
        for b in list(waiting):
            edge_from, rest_from = (blocks - b) % blocks, blocks - 1 - b
            if max(edge_from, rest_from) < len(mirrored):
                waiting.remove(b)
                there = pl.ds(half + b * lanes, lanes)
                out_ref[:, there] = jnp.where(edge, mirrored[edge_from], mirrored[rest_from])
                store(there)
    for copy in stores:
        copy.wait()


def cross_power(returned, source, second):
    width = returned.shape[1]
    count = second.shape[0]
    in_vmem = pl.BlockSpec(memory_space=pltpu.VMEM)
    return pl.pallas_call(
        power_kernel,
        in_specs=[in_vmem, in_vmem, in_vmem],
        out_specs=pl.BlockSpec(memory_space=pl.ANY),
        out_shape=pltpu.HBM((count, width), F32),
        scratch_shapes=[
            pltpu.VMEM((count, width), F32),
            pltpu.SemaphoreType.DMA((width // 256 // 2 + width // 128 // 2,)),
        ],
        compiler_params=pltpu.CompilerParams(vmem_limit_bytes=24 << 20),
        name="power",
    )(returned, source, second)


def exchange(packed, peers):
    rows, width = packed.shape
    moved = lax.all_to_all(
        packed.reshape(peers, rows // peers, width),
        ("tm", "cls"),
        split_axis=0,
        concat_axis=0,
        tiled=True,
    )
    return moved.reshape(rows, width)


def local(visibilities, row_class, filters, flags, taper, pairs):
    count = visibilities.shape[0]
    classes, width = filters.shape[0], filters.shape[1]
    peers = lax.axis_size(("tm", "cls"))
    rows = peers * TILE
    assert classes == 2 and count & (count - 1) == 0
    labels_row = row_class.reshape(1, count)
    in_hbm = lambda x: pltpu.with_memory_space_constraint(x, pltpu.HBM)
    packed = pack(in_hbm(labels_row), in_hbm(visibilities), rows, split_width(width, (1, 1, 1)))
    arrived = exchange(packed, peers)
    source, second = indices(labels_row, pairs.T)
    table = tapered_tables(width, taper.reshape(width, 1), 32)
    matrices = combine(in_hbm(filters), (1 - flags).astype(F32).T, table, 512)
    summed = filter_rows(arrived, in_hbm(matrices), split_width(width, (1, 2, 3)), 256)
    returned = exchange(summed, peers)
    return cross_power(returned, source, second)


def solution(mesh):
    across = ("tm", "cls")
    placed = (
        P(across, None),
        P(across, None),
        P(across, None, None),
        P(across, None),
        P(),
        P(across, None),
    )
    return jax.shard_map(
        local, mesh=mesh, in_specs=placed, out_specs=P(across, None), check_vma=False
    )
```

time: 118 us -> 117 us (level)
  Pallas kernels: 38 us -> 36.6 us
    pallas_call x3, Pallas kernels: 17.2 us -> 15.7 us  [the longest x1 7.81 us: filter_rows(): pl.pallas_call(functools.partial(filter_kernel, sizes, step), in_specs=[p...]
where the time goes in v3:
time: 117 us; the launch traced here: 116 us
  waiting for transfers between devices  58.2 us (50%)
  Pallas kernels  36.6 us (31%)
  starting transfers between devices  16.6 us (14%)
  local copies, waits for them, and re-layouts  3.5 us (3%)
    all_to_all x2, waiting for transfers between devices, exchange(): lax.all_to_all(packed.reshape(peers, rows // peers, width), ('tm', 'cls')...  58.2 us
    pallas_call x1, Pallas kernels, combine(): pl.pallas_call(combine_kernel, grid=(classes, width // step), in_specs=[b...  18.4 us
    all_to_all x2, starting transfers between devices, exchange(): lax.all_to_all(packed.reshape(peers, rows // peers, width), ('tm', 'cls')...  16.6 us
    pallas_call x1, Pallas kernels, filter_rows(): pl.pallas_call(functools.partial(filter_kernel, sizes, step), in_specs=[p...  7.81 us
    pallas_call x1, Pallas kernels, pack(): pl.pallas_call(functools.partial(pack_kernel, sizes), in_specs=[pl.BlockS...  4.45 us
    pallas_call x1, Pallas kernels, cross_power(): pl.pallas_call(power_kernel, in_specs=[in_vmem, in_vmem, in_vmem], out_sp...  3.46 us
  transfers between devices with their start and end apart: 2, of which 2 were waited for; matrix products, arithmetic and copies ran while one was open for 3% of the time, Pallas kernels for 18%

profile of v3, /device:TPU:4, one launch (start us, length us, event | category | flops | bytes accessed | tf_op | source)
XLA Modules:
  0.0 116.2 jit_solution(12671847449697468588)
XLA Ops:
  0.0 4.5 %pack.1 = bf16[1024,1536]{1,0:T(8,128)(2,1)} custom-call(s32[1,256]{1,0:T(1,128)} %bitcast.10, bf16[256,3072]{1,0:T(8,128)(2,1)} %rows_hbm.1), custom_call_target="tpu_custom_call" | custom-call | tf_op jit(solution)/shard_map/pack/pallas_call | solution.py:91
  4.5 0.0 copy-start.5
  4.5 0.0 copy-start.4
  4.5 10.5 %all-to-all-start = ((bf16[128,8,1536]{2,1,0:T(8,128)(2,1)}), bf16[128,8,1536]{2,1,0:T(8,128)(2,1)S(1)}, u32[]{:S(2)}, u32[]{:S(2)}) async-start(bf16[128,8,1536]{2,1,0:T(8,128)(2,1)} %bitcast.13), calls=%async_computation | async-start | bytes 6291456 | tf_op jit(solution)/shard_map/all_to_all | solution.py:350
  15.0 0.0 copy-done.5
  15.0 1.2 reshape.28.taper_ref
  16.2 0.0 copy-done.4
  16.2 1.2 %copy.12 = f32[2,1536]{0,1:T(8,128)} copy(f32[2,1536]{1,0:T(2,128)S(1)} %subtract_convert_fusion) | data formatting | bytes 24576 | tf_op jit(solution)/shard_map/convert_element_type | solution.py:372
  17.4 0.4 fusion.9
  17.8 0.0 copy-start
  17.8 0.7 sine_multiply_fusion
  18.5 0.0 copy-start.1
  18.5 1.1 copy-done.1
  19.6 2.2 %tables.1.table_ref = bf16[1536,1536]{1,0:T(8,128)(2,1)S(1)} custom-call(f32[48,768]{1,0:T(8,128)S(1)} %get-tuple-element.10.coarse_cos_ref, f32[48,768]{1,0:T(8,128)S(1)} %get-tuple-element.9.coarse_sin_ref, f32[32,768]{1,0:T(8,128)S(1)} %get-tuple-element.12.fine_cos_ref, f32[32,768]{1,0:T(8,128)S(1)} %get-tuple-element.11.fine_sin_ref, ...), custom_call_target="tpu_custom_call" | custom-call | tf_op jit(solution)/shard_map/tables/pallas_call | solution.py:165
  21.8 0.0 copy-done
  21.8 18.4 %combine.1.matrix_hbm = bf16[2,1536,1536]{2,1,0:T(8,128)(2,1)} custom-call(bf16[2,1536,1536]{2,1,0:T(8,128)(2,1)} %filters_ref.1, f32[1536,2]{1,0:T(8,128)S(1)} %bitcast.9, bf16[1536,1536]{1,0:T(8,128)(2,1)S(1)} %tables.1.table_ref), custom_call_target="tpu_custom_call" | custom-call | tf_op jit(solution)/shard_map/combine/pallas_call | solution.py:183
  40.2 16.7 %all-to-all-done = bf16[128,8,1536]{2,1,0:T(8,128)(2,1)S(1)} async-done(((bf16[128,8,1536]{2,1,0:T(8,128)(2,1)}), bf16[128,8,1536]{2,1,0:T(8,128)(2,1)S(1)}, u32[]{:S(2)}, u32[]{:S(2)}) %all-to-all-start) | async-done | bytes 3145760 | tf_op jit(solution)/shard_map/all_to_all | solution.py:350
  56.8 7.8 %filter.1 = bf16[1024,1536]{1,0:T(8,128)(2,1)} custom-call(bf16[1024,1536]{1,0:T(8,128)(2,1)S(1)} %bitcast.8, bf16[2,1536,1536]{2,1,0:T(8,128)(2,1)} %combine.1.matrix_hbm), custom_call_target="tpu_custom_call" | custom-call | tf_op jit(solution)/shard_map/filter/pallas_call | solution.py:244
  64.6 0.0 copy-start.2
  64.7 0.0 copy-start.3
  64.7 6.1 %all-to-all-start.1 = ((bf16[128,8,1536]{2,1,0:T(8,128)(2,1)}), bf16[128,8,1536]{2,1,0:T(8,128)(2,1)S(1)}, u32[]{:S(2)}, u32[]{:S(2)}) async-start(bf16[128,8,1536]{2,1,0:T(8,128)(2,1)} %bitcast.14), calls=%async_computation.1 | async-start | bytes 6291456 | tf_op jit(solution)/shard_map/all_to_all | solution.py:350
  70.8 0.0 copy-done.2
  70.8 0.0 copy-done.3
  70.8 0.3 indices.1
  71.1 41.5 %all-to-all-done.1 = bf16[128,8,1536]{2,1,0:T(8,128)(2,1)S(1)} async-done(((bf16[128,8,1536]{2,1,0:T(8,128)(2,1)}), bf16[128,8,1536]{2,1,0:T(8,128)(2,1)S(1)}, u32[]{:S(2)}, u32[]{:S(2)}) %all-to-all-start.1) | async-done | bytes 3145760 | tf_op jit(solution)/shard_map/all_to_all | solution.py:350
  112.6 3.5 %power.1 = f32[256,1536]{1,0:T(8,128)} custom-call(bf16[1024,1536]{1,0:T(8,128)(2,1)S(1)} %bitcast.7, s32[256,1]{1,0:T(8,128)S(1)} %get-tuple-element.7.source_ref, bf16[256,256]{1,0:T(8,128)(2,1)S(1)} %get-tuple-element.8.second_ref), custom_call_target="tpu_custom_call" | custom-call | tf_op jit(solution)/shard_map/power/pallas_call | solution.py:334
  (2 shorter events, 0.0 us)
Async XLA Ops:
  4.5 10.5 %copy-start.5 = (f32[1536]{0:T(1024)S(1)}, f32[1536]{0:T(1024)}, u32[]{:S(2)}) copy-start(f32[1536]{0:T(1024)} %param.10) | copy-start | bytes 18436
  4.5 11.7 %copy-start.4 = (s32[2,1536]{1,0:T(2,128)S(1)}, s32[2,1536]{1,0:T(2,128)}, u32[]{:S(2)}) copy-start(s32[2,1536]{1,0:T(2,128)} %param.9) | copy-start | bytes 36868
  4.5 52.4 %all-to-all-start = ((bf16[128,8,1536]{2,1,0:T(8,128)(2,1)}), bf16[128,8,1536]{2,1,0:T(8,128)(2,1)S(1)}, u32[]{:S(2)}, u32[]{:S(2)}) async-start(bf16[128,8,1536]{2,1,0:T(8,128)(2,1)} %bitcast.13), calls=%async_computation | async-start | bytes 6291456 | tf_op jit(solution)/shard_map/all_to_all | solution.py:350
  17.8 4.0 %copy-start = (f32[2,1536]{0,1:T(8,128)S(1)}, f32[2,1536]{0,1:T(8,128)}, u32[]{:S(2)}) copy-start(f32[2,1536]{0,1:T(8,128)} %copy.12) | copy-start | bytes 36868
  18.5 1.1 copy-start.1
  64.6 6.2 %copy-start.2 = (s32[256,1]{0,1:T(1,128)S(1)}, s32[256,1]{0,1:T(1,128)}, u32[]{:S(2)}) copy-start(s32[256,1]{0,1:T(1,128)} %param.7) | copy-start | bytes 3076
  64.7 6.1 %copy-start.3 = (s32[256,2]{0,1:T(2,128)S(1)}, s32[256,2]{0,1:T(2,128)}, u32[]{:S(2)}) copy-start(s32[256,2]{0,1:T(2,128)} %param.11) | copy-start | bytes 6148
  64.7 48.0 %all-to-all-start.1 = ((bf16[128,8,1536]{2,1,0:T(8,128)(2,1)}), bf16[128,8,1536]{2,1,0:T(8,128)(2,1)S(1)}, u32[]{:S(2)}, u32[]{:S(2)}) async-start(bf16[128,8,1536]{2,1,0:T(8,128)(2,1)} %bitcast.14), calls=%async_computation.1 | async-start | bytes 6291456 | tf_op jit(solution)/shard_map/all_to_all | solution.py:350

commit v4 on v3

--- a/solution.py
+++ b/solution.py
@@ -135,24 +135,36 @@
     )(labels_row, pairs_rows)
 
 
+def as_column(row):
+    lanes = 128
+    parts = [
+        jnp.broadcast_to(row[:, i : i + lanes], (lanes, lanes)).T[:, 0:1]
+        for i in range(0, row.shape[1], lanes)
+    ]
+    return jnp.concatenate(parts, axis=0)
+
+
 def table_kernel(coarse_cos_ref, coarse_sin_ref, fine_cos_ref, fine_sin_ref, taper_ref, out_ref):
     fine, half = fine_cos_ref.shape
     scale = 1.0 / math.sqrt(PARTS * half)
     fine_cos, fine_sin = fine_cos_ref[...], fine_sin_ref[...]
     start = iota((fine, half), 1) == 0
     turn = jnp.where(iota((fine, half), 0) & 1 == 0, scale, -scale)
-    for i in range(out_ref.shape[0] // fine):
+    taper = as_column(taper_ref[...])
+    for i in range(out_ref.shape[1] // fine):
         coarse_cos, coarse_sin = coarse_cos_ref[i : i + 1, :], coarse_sin_ref[i : i + 1, :]
         at = pl.ds(i * fine, fine)
-        taper = taper_ref[at, :]
-        cosines = (coarse_cos * fine_cos - coarse_sin * fine_sin).astype(BF16).astype(F32)
+        cosines = coarse_cos * fine_cos - coarse_sin * fine_sin
         sines = coarse_sin * fine_cos + coarse_cos * fine_sin
-        sines = jnp.where(start, turn, sines).astype(BF16).astype(F32)
-        out_ref[at, :half] = (cosines * taper).astype(BF16)
-        out_ref[at, half:] = (sines * taper).astype(BF16)
-
-
-def tapered_tables(width, taper_column, fine):
+        sines = jnp.where(start, turn, sines)
+        for table, columns in ((cosines, pl.ds(0, half)), (sines, pl.ds(half, half))):
+            tapered = table.astype(BF16).astype(F32) * taper[i * fine : (i + 1) * fine]
+            high = tapered.astype(BF16)
+            out_ref[0, at, columns] = high
+            out_ref[1, at, columns] = (tapered - high.astype(F32)).astype(BF16)
+
+
+def tapered_tables(width, taper_row, fine):
     half = width // 2
 
     def angles(rows, spacing):
@@ -164,20 +176,22 @@
     scale = 1.0 / math.sqrt(width)
     return pl.pallas_call(
         table_kernel,
-        out_shape=jax.ShapeDtypeStruct((width, width), BF16),
+        out_shape=jax.ShapeDtypeStruct((2, width, width), BF16),
         compiler_params=pltpu.CompilerParams(vmem_limit_bytes=24 << 20),
         name="tables",
-    )(jnp.cos(coarse) * scale, jnp.sin(coarse) * scale, jnp.cos(small), jnp.sin(small), taper_column)
-
-
-def combine_kernel(filters_ref, keep_ref, table_ref, out_ref):
-    which = pl.program_id(0)
-    keep = jnp.where(which == 0, keep_ref[:, 0:1], keep_ref[:, 1:2])
-    product = jnp.dot(filters_ref[0], table_ref[...], preferred_element_type=F32)
+    )(jnp.cos(coarse) * scale, jnp.sin(coarse) * scale, jnp.cos(small), jnp.sin(small), taper_row)
+
+
+def combine_kernel(filters_ref, flags_ref, table_ref, out_ref):
+    flags = jnp.where(pl.program_id(0) == 0, flags_ref[0:1, :], flags_ref[1:2, :])
+    keep = as_column((1 - flags).astype(F32))
+    matrix = filters_ref[0]
+    product = jnp.dot(matrix, table_ref[0], preferred_element_type=F32)
+    product = product + jnp.dot(matrix, table_ref[1], preferred_element_type=F32)
     out_ref[0] = (product * keep).astype(BF16)
 
 
-def combine(filters, keep_columns, table, step):
+def combine(filters, flags, table, step):
     classes, width, _ = filters.shape
     block = pl.BlockSpec((1, step, width), lambda w, i: (w, i, 0))
     return pl.pallas_call(
@@ -185,14 +199,14 @@
         grid=(classes, width // step),
         in_specs=[
             block,
-            pl.BlockSpec((step, classes), lambda w, i: (i, 0)),
-            pl.BlockSpec((width, width), lambda w, i: (0, 0), pipeline_mode=pl.Buffered(1)),
+            pl.BlockSpec((classes, step), lambda w, i: (0, i)),
+            pl.BlockSpec((2, width, width), lambda w, i: (0, 0, 0), pipeline_mode=pl.Buffered(1)),
         ],
         out_specs=block,
         out_shape=pltpu.HBM((classes, width, width), BF16),
-        compiler_params=pltpu.CompilerParams(vmem_limit_bytes=24 << 20),
+        compiler_params=pltpu.CompilerParams(vmem_limit_bytes=36 << 20),
         name="combine",
-    )(filters, keep_columns, table)
+    )(filters, flags, table)
 
 
 def filter_kernel(sizes, step, arrived_ref, matrix_hbm, out_hbm, split_ref, matrix_ref, out_ref, in_sems, out_sems):
@@ -368,8 +382,8 @@
     packed = pack(in_hbm(labels_row), in_hbm(visibilities), rows, split_width(width, (1, 1, 1)))
     arrived = exchange(packed, peers)
     source, second = indices(labels_row, pairs.T)
-    table = tapered_tables(width, taper.reshape(width, 1), 32)
-    matrices = combine(in_hbm(filters), (1 - flags).astype(F32).T, table, 512)
+    table = tapered_tables(width, taper.reshape(1, width), 32)
+    matrices = combine(in_hbm(filters), flags, table, 512)
     summed = filter_rows(arrived, in_hbm(matrices), split_width(width, (1, 2, 3)), 256)
     returned = exchange(summed, peers)
     return cross_power(returned, source, second)

time: 117 us -> 117 us (level)
  Pallas kernels: 36.6 us -> 52.2 us
  waiting for transfers between devices: 58.2 us -> 45.9 us
  local copies, waits for them, and re-layouts: 3.5 us -> 0.03 us
    pallas_call x1, Pallas kernels: 18.4 us -> 32.9 us  [combine(): pl.pallas_call(combine_kernel, grid=(classes, width // step), in_specs=[b...]
    all_to_all x2, waiting for transfers between devices: 58.2 us -> 45.9 us  [exchange(): lax.all_to_all(packed.reshape(peers, rows // peers, width), ('tm', 'cls')...]
    convert_element_type x1 -> x0, local copies, waits for them, and re-layouts: 1.18 us -> none  [local(): matrices = combine(in_hbm(filters), (1 - flags).astype(F32).T, table, 512)]
  transfers between devices with their start and end apart: 2 -> 2, of which waited for: 2 -> 2; matrix products, arithmetic and copies ran while one was open for 3% -> 1% of each run, Pallas kernels for 18% -> 31%
where the time goes in v4:
time: 117 us; the launch traced here: 116 us
  Pallas kernels  52.2 us (45%)
  waiting for transfers between devices  45.9 us (39%)
  starting transfers between devices  16.6 us (14%)
    all_to_all x2, waiting for transfers between devices, exchange(): lax.all_to_all(packed.reshape(peers, rows // peers, width), ('tm', 'cls')...  45.9 us
    pallas_call x1, Pallas kernels, combine(): pl.pallas_call(combine_kernel, grid=(classes, width // step), in_specs=[b...  32.9 us
    all_to_all x2, starting transfers between devices, exchange(): lax.all_to_all(packed.reshape(peers, rows // peers, width), ('tm', 'cls')...  16.6 us
    pallas_call x1, Pallas kernels, filter_rows(): pl.pallas_call(functools.partial(filter_kernel, sizes, step), in_specs=[p...  7.78 us
    pallas_call x1, Pallas kernels, pack(): pl.pallas_call(functools.partial(pack_kernel, sizes), in_specs=[pl.BlockS...  4.41 us
    pallas_call x1, Pallas kernels, cross_power(): pl.pallas_call(power_kernel, in_specs=[in_vmem, in_vmem, in_vmem], out_sp...  3.46 us
    pallas_call x1, Pallas kernels, tapered_tables(): pl.pallas_call(table_kernel, out_shape=jax.ShapeDtypeStruct((2, width, wi...  3.29 us
  transfers between devices with their start and end apart: 2, of which 2 were waited for; matrix products, arithmetic and copies ran while one was open for 1% of the time, Pallas kernels for 31%

profile of v4, /device:TPU:4, one launch (start us, length us, event | category | flops | bytes accessed | tf_op | source)
XLA Modules:
  0.0 116.2 jit_solution(567153273223766428)
XLA Ops:
  0.0 4.4 %pack.1 = bf16[1024,1536]{1,0:T(8,128)(2,1)} custom-call(s32[1,256]{1,0:T(1,128)} %bitcast.8, bf16[256,3072]{1,0:T(8,128)(2,1)} %rows_hbm.1), custom_call_target="tpu_custom_call" | custom-call | tf_op jit(solution)/shard_map/pack/pallas_call | solution.py:91
  4.4 0.0 copy-start.3
  4.4 10.5 %all-to-all-start = ((bf16[128,8,1536]{2,1,0:T(8,128)(2,1)}), bf16[128,8,1536]{2,1,0:T(8,128)(2,1)S(1)}, u32[]{:S(2)}, u32[]{:S(2)}) async-start(bf16[128,8,1536]{2,1,0:T(8,128)(2,1)} %bitcast.11), calls=%async_computation | async-start | bytes 6291456 | tf_op jit(solution)/shard_map/all_to_all | solution.py:364
  14.9 0.0 copy-done.3
  15.0 0.4 fusion.9
  15.4 0.7 sine_multiply_fusion
  16.1 0.0 copy-start
  16.1 3.3 %tables.1.table_ref = bf16[2,1536,1536]{2,1,0:T(8,128)(2,1)S(1)} custom-call(f32[48,768]{1,0:T(8,128)S(1)} %get-tuple-element.10.coarse_cos_ref, f32[48,768]{1,0:T(8,128)S(1)} %get-tuple-element.9.coarse_sin_ref, f32[32,768]{1,0:T(8,128)S(1)} %get-tuple-element.12.fine_cos_ref, f32[32,768]{1,0:T(8,128)S(1)} %get-tuple-element.11.fine_sin_ref, ...), custom_call_target="tpu_custom_call" | custom-call | tf_op jit(solution)/shard_map/tables/pallas_call | solution.py:177
  19.4 0.0 copy-done
  19.4 32.9 %combine.1.matrix_hbm = bf16[2,1536,1536]{2,1,0:T(8,128)(2,1)} custom-call(bf16[2,1536,1536]{2,1,0:T(8,128)(2,1)} %filters_ref.1, s32[2,1536]{1,0:T(2,128)S(1)} %copy-done, bf16[2,1536,1536]{2,1,0:T(8,128)(2,1)S(1)} %tables.1.table_ref), custom_call_target="tpu_custom_call" | custom-call | tf_op jit(solution)/shard_map/combine/pallas_call | solution.py:197
  52.4 4.4 %all-to-all-done = bf16[128,8,1536]{2,1,0:T(8,128)(2,1)S(1)} async-done(((bf16[128,8,1536]{2,1,0:T(8,128)(2,1)}), bf16[128,8,1536]{2,1,0:T(8,128)(2,1)S(1)}, u32[]{:S(2)}, u32[]{:S(2)}) %all-to-all-start) | async-done | bytes 3145760 | tf_op jit(solution)/shard_map/all_to_all | solution.py:364
  56.8 7.8 %filter.1 = bf16[1024,1536]{1,0:T(8,128)(2,1)} custom-call(bf16[1024,1536]{1,0:T(8,128)(2,1)S(1)} %bitcast.7, bf16[2,1536,1536]{2,1,0:T(8,128)(2,1)} %combine.1.matrix_hbm), custom_call_target="tpu_custom_call" | custom-call | tf_op jit(solution)/shard_map/filter/pallas_call | solution.py:258
  64.6 0.0 copy-start.1
  64.6 0.0 copy-start.2
  64.6 6.1 %all-to-all-start.1 = ((bf16[128,8,1536]{2,1,0:T(8,128)(2,1)}), bf16[128,8,1536]{2,1,0:T(8,128)(2,1)S(1)}, u32[]{:S(2)}, u32[]{:S(2)}) async-start(bf16[128,8,1536]{2,1,0:T(8,128)(2,1)} %bitcast.12), calls=%async_computation.1 | async-start | bytes 6291456 | tf_op jit(solution)/shard_map/all_to_all | solution.py:364
  70.7 0.0 copy-done.1
  70.7 0.0 copy-done.2
  70.7 0.3 indices.1
  71.0 41.5 %all-to-all-done.1 = bf16[128,8,1536]{2,1,0:T(8,128)(2,1)S(1)} async-done(((bf16[128,8,1536]{2,1,0:T(8,128)(2,1)}), bf16[128,8,1536]{2,1,0:T(8,128)(2,1)S(1)}, u32[]{:S(2)}, u32[]{:S(2)}) %all-to-all-start.1) | async-done | bytes 3145760 | tf_op jit(solution)/shard_map/all_to_all | solution.py:364
  112.6 3.5 %power.1 = f32[256,1536]{1,0:T(8,128)} custom-call(bf16[1024,1536]{1,0:T(8,128)(2,1)S(1)} %bitcast.6, s32[256,1]{1,0:T(8,128)S(1)} %get-tuple-element.7.source_ref, bf16[256,256]{1,0:T(8,128)(2,1)S(1)} %get-tuple-element.8.second_ref), custom_call_target="tpu_custom_call" | custom-call | tf_op jit(solution)/shard_map/power/pallas_call | solution.py:348
  (2 shorter events, 0.0 us)
Async XLA Ops:
  4.4 10.5 %copy-start.3 = (f32[1536]{0:T(1024)S(1)}, f32[1536]{0:T(1024)}, u32[]{:S(2)}) copy-start(f32[1536]{0:T(1024)} %param.10) | copy-start | bytes 18436
  4.4 52.4 %all-to-all-start = ((bf16[128,8,1536]{2,1,0:T(8,128)(2,1)}), bf16[128,8,1536]{2,1,0:T(8,128)(2,1)S(1)}, u32[]{:S(2)}, u32[]{:S(2)}) async-start(bf16[128,8,1536]{2,1,0:T(8,128)(2,1)} %bitcast.11), calls=%async_computation | async-start | bytes 6291456 | tf_op jit(solution)/shard_map/all_to_all | solution.py:364
  16.1 3.3 %copy-start = (s32[2,1536]{1,0:T(2,128)S(1)}, s32[2,1536]{1,0:T(2,128)}, u32[]{:S(2)}) copy-start(s32[2,1536]{1,0:T(2,128)} %flags_ref.1) | copy-start | bytes 36868
  64.6 6.1 %copy-start.1 = (s32[256,1]{0,1:T(1,128)S(1)}, s32[256,1]{0,1:T(1,128)}, u32[]{:S(2)}) copy-start(s32[256,1]{0,1:T(1,128)} %param.7) | copy-start | bytes 3076
  64.6 6.1 %copy-start.2 = (s32[256,2]{0,1:T(2,128)S(1)}, s32[256,2]{0,1:T(2,128)}, u32[]{:S(2)}) copy-start(s32[256,2]{0,1:T(2,128)} %param.11) | copy-start | bytes 6148
  64.6 48.0 %all-to-all-start.1 = ((bf16[128,8,1536]{2,1,0:T(8,128)(2,1)}), bf16[128,8,1536]{2,1,0:T(8,128)(2,1)S(1)}, u32[]{:S(2)}, u32[]{:S(2)}) async-start(bf16[128,8,1536]{2,1,0:T(8,128)(2,1)} %bitcast.12), calls=%async_computation.1 | async-start | bytes 6291456 | tf_op jit(solution)/shard_map/all_to_all | solution.py:364

commit v5 on v4

--- a/solution.py
+++ b/solution.py
@@ -13,6 +13,7 @@
 SLOTS = 2
 PARTS = 2
 TILE = 8
+PACKED = 16
 
 
 def iota(shape, axis):
@@ -30,16 +31,19 @@
     down = across.T
     earlier = iota((count, count), 0) < iota((count, count), 1)
     place = jnp.sum(jnp.where((across == down) & earlier, 1.0, 0.0), axis=0, keepdims=True)
-    return labels_row * SLOTS + place.astype(jnp.int32)
-
-
-def weave(first, second):
+    swap = (lax.axis_index("cls") >> 1) & 1
+    return (labels_row ^ swap) * SLOTS + place.astype(jnp.int32)
+
+
+def row_of_slot(slots):
+    return (slots & ~12) | ((slots & 4) << 1) | ((slots & 8) >> 1)
+
+
+def alternate(first, second, own, group):
     rows, width = first.shape
-    groups = (rows // TILE, TILE, width)
+    groups = (rows // group, group, width)
     first, second = first.reshape(groups), second.reshape(groups)
-    low = iota((1, TILE, 1), 1) < TILE // 2
-    even = jnp.where(low, first, pltpu.roll(second, TILE // 2, 1))
-    odd = jnp.where(low, pltpu.roll(first, TILE // 2, 1), second)
+    even, odd = jnp.where(own, first, second), jnp.where(own, second, first)
     return jnp.concatenate([even[:, None], odd[:, None]], axis=1).reshape(2 * rows, width)
 
 
@@ -69,17 +73,21 @@
     for pair in loads:
         for load in pair:
             load.start()
-    select_ref[...] = jnp.where(
-        iota(select_ref.shape, 0) == slot_of_row(labels_ref[...]), 1.0, 0.0
-    ).astype(BF16)
+    each = TILE // PARTS
+    row = row_of_slot(slot_of_row(labels_ref[...]))
+    index = iota(select_ref.shape[1:], 0)
+    for part in range(PARTS):
+        chosen = index == row ^ (part * each)
+        select_ref[part] = jnp.where(chosen, 1.0, 0.0).astype(BF16)
+    own = iota((1, PACKED, 1), 1) & each == 0
     for j, at in enumerate(columns):
         for load in loads[j]:
             load.wait()
         parts = [
-            jnp.dot(select_ref[...], rows_ref[part, :, at], preferred_element_type=F32)
+            jnp.dot(select_ref[part], rows_ref[part, :, at], preferred_element_type=F32)
             for part in range(PARTS)
         ]
-        out_ref[:, at] = weave(*parts).astype(BF16)
+        out_ref[:, at] = alternate(*parts, own, PACKED).astype(BF16)
         stores[j].start()
     for store in stores:
         store.wait()
@@ -95,7 +103,7 @@
         out_shape=pltpu.HBM((rows, width), BF16),
         scratch_shapes=[
             pltpu.VMEM((PARTS, count, width), BF16),
-            pltpu.VMEM((rows // PARTS, count), BF16),
+            pltpu.VMEM((PARTS, rows // PARTS, count), BF16),
             pltpu.VMEM((rows, width), BF16),
             pltpu.SemaphoreType.DMA((PARTS, len(sizes))),
             pltpu.SemaphoreType.DMA((len(sizes),)),
@@ -107,9 +115,7 @@
 
 def index_kernel(labels_ref, pairs_ref, source_ref, second_ref):
     count = labels_ref.shape[1]
-    slots = slot_of_row(labels_ref[...])
-    each = TILE // PARTS
-    place = slots // each * TILE + slots % each
+    place = row_of_slot(slot_of_row(labels_ref[...]))
     local = (pairs_ref[...] & (count - 1)).astype(F32)
     first = jnp.broadcast_to(local[0:1], (count, count))
     other = jnp.broadcast_to(local[1:2], (count, count))
@@ -216,18 +222,17 @@
         pltpu.make_async_copy(matrix_hbm.at[:, :, at], matrix_ref.at[:, :, at], in_sems.at[j])
         for j, at in enumerate(columns)
     ]
-    own = iota((1, TILE, 1), 1) & SLOTS == 0
+    own = iota((1, PACKED, 1), 1) & SLOTS == 0
     loads[0].start()
     groups = len(loads) - 1
     count = rows // (2 * groups)
     for g in range(groups):
-        arrived = arrived_ref[pl.ds(2 * g * count, 2 * count), :].astype(F32)
-        arrived = arrived.reshape(count // TILE, 2, TILE, width)
+        arrived = arrived_ref[pl.ds(2 * g * count, 2 * count), :]
+        arrived = arrived.reshape(count // PACKED, 2, PACKED, width)
         even, odd = arrived[:, 0], arrived[:, 1]
-        first = jnp.where(own, even, pltpu.roll(odd, SLOTS, 1))
-        second = jnp.where(own, pltpu.roll(even, TILE - SLOTS, 1), odd)
-        split_ref[0, pl.ds(g * count, count), :] = first.reshape(count, width).astype(BF16)
-        split_ref[1, pl.ds(g * count, count), :] = second.reshape(count, width).astype(BF16)
+        first, second = jnp.where(own, even, odd), jnp.where(own, odd, even)
+        split_ref[0, pl.ds(g * count, count), :] = first.reshape(count, width)
+        split_ref[1, pl.ds(g * count, count), :] = second.reshape(count, width)
         loads[g + 1].start()
     stores = []
     for load, piece in zip(loads, columns):
@@ -236,13 +241,9 @@
             at = pl.ds(start, step)
             done = [
                 jnp.dot(split_ref[w], matrix_ref[w, :, at], preferred_element_type=F32)
-                .reshape(rows // (2 * TILE), TILE, step)
                 for w in range(2)
             ]
-            even = jnp.where(own, done[0], pltpu.roll(done[1], SLOTS, 1))
-            odd = jnp.where(own, pltpu.roll(done[0], TILE - SLOTS, 1), done[1])
-            both = jnp.concatenate([even[:, None], odd[:, None]], axis=1)
-            out_ref[:, at] = both.reshape(rows, step).astype(BF16)
+            out_ref[:, at] = alternate(*done, own, PACKED).astype(BF16)
             store = pltpu.make_async_copy(
                 out_ref.at[:, at], out_hbm.at[:, at], out_sems.at[len(stores)]
             )
@@ -277,14 +278,23 @@
     rows, width = returned_ref.shape
     half, lanes, step = width // 2, 128, 256
     second = second_ref[...]
-    index = iota((count, rows), 1)
-    fetch = jnp.concatenate(
-        [
-            jnp.where(index == source_ref[...] + part * (TILE // PARTS), 1.0, 0.0).astype(BF16)
-            for part in range(PARTS)
-        ],
-        axis=0,
-    )
+    each = TILE // PARTS
+    index = iota((count, rows // PARTS), 1)
+    fetch = [
+        jnp.where(index == source_ref[...] ^ (part * each), 1.0, 0.0).astype(BF16)
+        for part in range(PARTS)
+    ]
+    own = iota((1, PACKED, 1), 1) & each == 0
+
+    def fetched(at):
+        groups = returned_ref[:, at].reshape(rows // (2 * PACKED), 2, PACKED, step)
+        even, odd = groups[:, 0], groups[:, 1]
+        parts = [jnp.where(own, even, odd), jnp.where(own, odd, even)]
+        return [
+            jnp.dot(chosen, part.reshape(-1, step), preferred_element_type=F32)
+            for chosen, part in zip(fetch, parts)
+        ]
+
     mirror = (lanes - iota((count, lanes), 1)) & (lanes - 1)
     start = iota((count, step), 1) == 0
     edge = iota((count, lanes), 1) == 0
@@ -314,9 +324,7 @@
     for j in range(half // step):
         at = pl.ds(j * step, step)
         far_at = pl.ds(half + j * step, step)
-        cos_sum = jnp.dot(fetch, returned_ref[:, at], preferred_element_type=F32)
-        sin_sum = jnp.dot(fetch, returned_ref[:, far_at], preferred_element_type=F32)
-        sums = [cos_sum[:count], cos_sum[count:], sin_sum[:count], sin_sum[count:]]
+        sums = fetched(at) + fetched(far_at)
         others = jnp.dot(
             second, jnp.concatenate(sums, axis=1).astype(BF16), preferred_element_type=F32
         )

time: 117 us -> 115 us (0.983)
  transfers between devices with their start and end apart: 2 -> 2, of which waited for: 2 -> 2; matrix products, arithmetic and copies ran while one was open for 1% -> 1% of each run, Pallas kernels for 31% -> 32%
where the time goes in v5:
time: 115 us
  Pallas kernels  51.2 us (45%)
  waiting for transfers between devices  45.9 us (40%)
  starting transfers between devices  16.6 us (14%)
    all_to_all x2, waiting for transfers between devices, exchange(): lax.all_to_all(packed.reshape(peers, rows // peers, width), ('tm', 'cls')...  45.9 us
    pallas_call x1, Pallas kernels, combine(): pl.pallas_call(combine_kernel, grid=(classes, width // step), in_specs=[b...  32.9 us
    all_to_all x2, starting transfers between devices, exchange(): lax.all_to_all(packed.reshape(peers, rows // peers, width), ('tm', 'cls')...  16.6 us
    pallas_call x1, Pallas kernels, filter_rows(): pl.pallas_call(functools.partial(filter_kernel, sizes, step), in_specs=[p...  7.71 us
    pallas_call x1, Pallas kernels, pack(): pl.pallas_call(functools.partial(pack_kernel, sizes), in_specs=[pl.BlockS...  4.14 us
    pallas_call x1, Pallas kernels, tapered_tables(): pl.pallas_call(table_kernel, out_shape=jax.ShapeDtypeStruct((2, width, wi...  3.29 us
    pallas_call x1, Pallas kernels, cross_power(): pl.pallas_call(power_kernel, in_specs=[in_vmem, in_vmem, in_vmem], out_sp...  2.77 us
  transfers between devices with their start and end apart: 2, of which 2 were waited for; matrix products, arithmetic and copies ran while one was open for 1% of the time, Pallas kernels for 32%

profile of v5, /device:TPU:4, one launch (start us, length us, event | category | flops | bytes accessed | tf_op | source)
XLA Modules:
  0.0 115.0 jit_solution(7193478650464004538)
XLA Ops:
  0.0 4.1 %pack.1 = bf16[1024,1536]{1,0:T(8,128)(2,1)} custom-call(s32[1,256]{1,0:T(1,128)} %bitcast.8, bf16[256,3072]{1,0:T(8,128)(2,1)} %rows_hbm.1), custom_call_target="tpu_custom_call" | custom-call | tf_op jit(solution)/shard_map/pack/pallas_call | solution.py:99
  4.2 0.0 copy-start.3
  4.2 10.5 %all-to-all-start = ((bf16[128,8,1536]{2,1,0:T(8,128)(2,1)}), bf16[128,8,1536]{2,1,0:T(8,128)(2,1)S(1)}, u32[]{:S(2)}, u32[]{:S(2)}) async-start(bf16[128,8,1536]{2,1,0:T(8,128)(2,1)} %bitcast.11), calls=%async_computation | async-start | bytes 6291456 | tf_op jit(solution)/shard_map/all_to_all | solution.py:372
  14.7 0.0 copy-done.3
  14.7 0.4 fusion.9
  15.1 0.7 sine_multiply_fusion
  15.8 0.0 copy-start
  15.8 3.3 %tables.1.table_ref = bf16[2,1536,1536]{2,1,0:T(8,128)(2,1)S(1)} custom-call(f32[48,768]{1,0:T(8,128)S(1)} %get-tuple-element.10.coarse_cos_ref, f32[48,768]{1,0:T(8,128)S(1)} %get-tuple-element.9.coarse_sin_ref, f32[32,768]{1,0:T(8,128)S(1)} %get-tuple-element.12.fine_cos_ref, f32[32,768]{1,0:T(8,128)S(1)} %get-tuple-element.11.fine_sin_ref, ...), custom_call_target="tpu_custom_call" | custom-call | tf_op jit(solution)/shard_map/tables/pallas_call | solution.py:183
  19.1 0.0 copy-done
  19.1 32.9 %combine.1.matrix_hbm = bf16[2,1536,1536]{2,1,0:T(8,128)(2,1)} custom-call(bf16[2,1536,1536]{2,1,0:T(8,128)(2,1)} %filters_ref.1, s32[2,1536]{1,0:T(2,128)S(1)} %copy-done, bf16[2,1536,1536]{2,1,0:T(8,128)(2,1)S(1)} %tables.1.table_ref), custom_call_target="tpu_custom_call" | custom-call | tf_op jit(solution)/shard_map/combine/pallas_call | solution.py:203
  52.1 4.4 %all-to-all-done = bf16[128,8,1536]{2,1,0:T(8,128)(2,1)S(1)} async-done(((bf16[128,8,1536]{2,1,0:T(8,128)(2,1)}), bf16[128,8,1536]{2,1,0:T(8,128)(2,1)S(1)}, u32[]{:S(2)}, u32[]{:S(2)}) %all-to-all-start) | async-done | bytes 3145760 | tf_op jit(solution)/shard_map/all_to_all | solution.py:372
  56.5 7.7 %filter.1 = bf16[1024,1536]{1,0:T(8,128)(2,1)} custom-call(bf16[1024,1536]{1,0:T(8,128)(2,1)S(1)} %bitcast.7, bf16[2,1536,1536]{2,1,0:T(8,128)(2,1)} %combine.1.matrix_hbm), custom_call_target="tpu_custom_call" | custom-call | tf_op jit(solution)/shard_map/filter/pallas_call | solution.py:259
  64.2 0.0 copy-start.1
  64.2 0.0 copy-start.2
  64.3 6.1 %all-to-all-start.1 = ((bf16[128,8,1536]{2,1,0:T(8,128)(2,1)}), bf16[128,8,1536]{2,1,0:T(8,128)(2,1)S(1)}, u32[]{:S(2)}, u32[]{:S(2)}) async-start(bf16[128,8,1536]{2,1,0:T(8,128)(2,1)} %bitcast.12), calls=%async_computation.1 | async-start | bytes 6291456 | tf_op jit(solution)/shard_map/all_to_all | solution.py:372
  70.4 0.0 copy-done.1
  70.4 0.0 copy-done.2
  70.4 0.3 indices.1
  70.7 41.5 %all-to-all-done.1 = bf16[128,8,1536]{2,1,0:T(8,128)(2,1)S(1)} async-done(((bf16[128,8,1536]{2,1,0:T(8,128)(2,1)}), bf16[128,8,1536]{2,1,0:T(8,128)(2,1)S(1)}, u32[]{:S(2)}, u32[]{:S(2)}) %all-to-all-start.1) | async-done | bytes 3145760 | tf_op jit(solution)/shard_map/all_to_all | solution.py:372
  112.2 2.8 %power.1 = f32[256,1536]{1,0:T(8,128)} custom-call(bf16[1024,1536]{1,0:T(8,128)(2,1)S(1)} %bitcast.6, s32[256,1]{1,0:T(8,128)S(1)} %get-tuple-element.7.source_ref, bf16[256,256]{1,0:T(8,128)(2,1)S(1)} %get-tuple-element.8.second_ref), custom_call_target="tpu_custom_call" | custom-call | tf_op jit(solution)/shard_map/power/pallas_call | solution.py:356
  (2 shorter events, 0.0 us)
Async XLA Ops:
  4.2 10.5 %copy-start.3 = (f32[1536]{0:T(1024)S(1)}, f32[1536]{0:T(1024)}, u32[]{:S(2)}) copy-start(f32[1536]{0:T(1024)} %param.10) | copy-start | bytes 18436
  4.2 52.4 %all-to-all-start = ((bf16[128,8,1536]{2,1,0:T(8,128)(2,1)}), bf16[128,8,1536]{2,1,0:T(8,128)(2,1)S(1)}, u32[]{:S(2)}, u32[]{:S(2)}) async-start(bf16[128,8,1536]{2,1,0:T(8,128)(2,1)} %bitcast.11), calls=%async_computation | async-start | bytes 6291456 | tf_op jit(solution)/shard_map/all_to_all | solution.py:372
  15.8 3.3 %copy-start = (s32[2,1536]{1,0:T(2,128)S(1)}, s32[2,1536]{1,0:T(2,128)}, u32[]{:S(2)}) copy-start(s32[2,1536]{1,0:T(2,128)} %flags_ref.1) | copy-start | bytes 36868
  64.2 6.1 %copy-start.1 = (s32[256,1]{0,1:T(1,128)S(1)}, s32[256,1]{0,1:T(1,128)}, u32[]{:S(2)}) copy-start(s32[256,1]{0,1:T(1,128)} %param.7) | copy-start | bytes 3076
  64.2 6.1 %copy-start.2 = (s32[256,2]{0,1:T(2,128)S(1)}, s32[256,2]{0,1:T(2,128)}, u32[]{:S(2)}) copy-start(s32[256,2]{0,1:T(2,128)} %param.11) | copy-start | bytes 6148
  64.3 48.0 %all-to-all-start.1 = ((bf16[128,8,1536]{2,1,0:T(8,128)(2,1)}), bf16[128,8,1536]{2,1,0:T(8,128)(2,1)S(1)}, u32[]{:S(2)}, u32[]{:S(2)}) async-start(bf16[128,8,1536]{2,1,0:T(8,128)(2,1)} %bitcast.12), calls=%async_computation.1 | async-start | bytes 6291456 | tf_op jit(solution)/shard_map/all_to_all | solution.py:372
